TPU v7x, 128 devices: a whole 4x4x4 slice. The times are simulated.
128 devices in a mesh: row: 8 (over z, core), col: 16 (over x, y).
Axes of the slice: x: 4, y: 4, z: 4, core: 2. Of those that a mesh axis runs over, the one named last changes fastest.
Arguments:
- colloc_points: float32 [3, 61440], P(None, 'row'), may hold values from -1 to 1, as said below
- sources: float32 [4, 2048], P(None, 'col'), may hold values from -1 to 1, as said below
- counts: int32 [480, 16], P('row', 'col'), may hold values from 2 to 16, as said below
- row_element: int32 [61440], P('row'), may hold values from 0 to 61439, as said below
- pivots: int32 [128], replicated, may hold values from 0 to 61439, as said below
Outputs:
- factored: float32 [61440, 2048], P('row', 'col')
- u_rows: float32 [128, 2048], P(None, 'col')
Inputs may be any that keep to these rules, and one draw needn't show every extreme that they name: `counts`: every tile uses 2 to 16 quadrature points, and some tile uses 16. `row_element`: a permutation of the 61440 elements. pivots[k] is the row r with row_element[r] == k. `colloc_points`: first two coordinates between 0 and 1, third between -0.1 and 0.1. `sources`: centres as for the collocation points; core radii between 0.05 and 0.15.
All inputs are finite; a program needn't handle non-finite values.
Results may differ from a plain program's by a relative error of at most 0.0003.
Values sent between devices are 32-bit elements; how exact they have to be, the bound alone decides.
No kernel may reach another device: no remote copies, remote signals or barrier semaphores. Data moves between devices by JAX's collectives and lax.ppermute only.
A program may use at most 64 MiB of HBM per device.

v0:
```python
import functools

import jax
import jax.numpy as jnp
import numpy as np
from jax import lax
from jax.experimental import pallas as pl
from jax.experimental.pallas import tpu as pltpu
from jax.sharding import PartitionSpec as P


F32 = jnp.float32
BF = jnp.bfloat16
I32 = jnp.int32

TILE = 128
QUAD_MAX = 16
PAIRS = QUAD_MAX // 2
FEATS = 32
JUMP = 512.0
BLOCK = 16
GROUP = 10
JOBS = 8


def split3(v):
    high = v.astype(BF).astype(F32)
    rest = v - high
    mid = rest.astype(BF).astype(F32)
    low = (rest - mid).astype(BF).astype(F32)
    return high, mid, low


def mm(a, b):
    return jnp.dot(a, b, preferred_element_type=F32)


def halves(v):
    high = v.astype(BF)
    return high, (v - high.astype(F32)).astype(BF)


def mm3(a_high, a_low, b):
    b_high, b_low = halves(b)
    both = jnp.concatenate([a_high, a_low], 1)
    return mm(both, jnp.concatenate([b_high, b_high], 0)) + mm(a_high, b_low)


def point_features(x, y, z, extra):
    xs = x - 0.5
    ys = y - 0.5
    rows = []
    for v in (xs, ys, z):
        h, m, l = split3(v)
        rows += [h, h, m, m, h, l]
    rows += list(split3(xs * xs + ys * ys + z * z))
    one = jnp.ones_like(x)
    rows += [one, one, one]
    rows += extra
    zero = jnp.zeros_like(x)
    rows += [zero] * (FEATS - len(rows))
    rows = jnp.concatenate(rows, 0)
    return jnp.concatenate([rows, jnp.zeros((TILE - FEATS, TILE), F32)], 0)


def quad_offsets():
    numbers = np.arange(QUAD_MAX).astype(np.float32)
    radius = np.float32(4.0) * np.sqrt((numbers + np.float32(0.5)) / np.float32(QUAD_MAX))
    angles = np.float32(2.39996323) * numbers
    return radius * np.cos(angles), radius * np.sin(angles)


def build_table(s, wide_ref, tab_ref):
    off_x, off_y = quad_offsets()
    numbers = lax.broadcasted_iota(I32, (QUAD_MAX, TILE), 0)
    ox = jnp.zeros((QUAD_MAX, TILE), F32)
    oy = ox
    for q in range(QUAD_MAX):
        ox = jnp.where(numbers == q, float(off_x[q]), ox)
        oy = jnp.where(numbers == q, float(off_y[q]), oy)
    sx, sy, sz, size = [jnp.broadcast_to(s[i : i + 1], (QUAD_MAX, TILE)) for i in range(4)]
    ux = (sx + size * ox) - 0.5
    uy = (sy + size * oy) - 0.5
    norm = ux * ux + uy * uy + sz * sz + size * size
    wide_ref[...] = jnp.zeros_like(wide_ref)

    def put(f, v):
        wide_ref[pl.ds(f, QUAD_MAX, stride=FEATS), :] = v

    for base, u in ((0, -2.0 * ux), (6, -2.0 * uy), (12, -2.0 * sz)):
        uh, um, ul = split3(u)
        for k, v in enumerate((uh, um, uh, um, ul, uh)):
            put(base + k, v)
    one = jnp.ones((QUAD_MAX, TILE), F32)
    for k in range(3):
        put(18 + k, one)
    for k, v in enumerate(split3(norm)):
        put(21 + k, v)
    tab_ref[...] = jnp.zeros_like(tab_ref)
    rows = lax.broadcasted_iota(I32, (FEATS, TILE), 0)
    far = jnp.where(rows == 21, 1e30, 0.0).astype(BF)
    for q in range(QUAD_MAX):
        block = wide_ref[pl.ds(FEATS * q, FEATS), :].astype(BF)
        j = q // 2
        if q % 2 == 0:
            tab_ref[j, 0:FEATS, 0:TILE] = block
            tab_ref[PAIRS + j, 0:FEATS, 0:TILE] = block
            tab_ref[PAIRS + j, 0:FEATS, TILE:] = far
        else:
            tab_ref[j, 0:FEATS, TILE:] = block
    tab_ref[2 * PAIRS, 0:FEATS, 0:TILE] = far
    tab_ref[2 * PAIRS, 0:FEATS, TILE:] = far


def depth_rows(s):
    rows = lax.broadcasted_iota(I32, (FEATS, TILE), 0)
    zh, zm, zl = split3(jnp.broadcast_to(s[2:3], (FEATS, TILE)))
    dz = jnp.where((rows == 12) | (rows == 14) | (rows == 17), 1.0, 0.0)
    dz = jnp.where(rows == 21, -zh, dz)
    dz = jnp.where(rows == 22, -zm, dz)
    return jnp.where(rows == 23, -zl, dz)


def build_side(s, first_col, side_ref):
    rows = lax.broadcasted_iota(I32, (FEATS, TILE), 0)
    ids = (lax.broadcasted_iota(I32, (FEATS, TILE), 1) + first_col).astype(F32)
    high = jnp.floor(ids * (1.0 / 256.0))
    low = ids - 256.0 * high
    e = jnp.where(rows == 24, 256.0, 0.0)
    e = jnp.where(rows == 25, 1.0, e)
    e = jnp.where(rows == 21, -256.0 * high, e)
    e = jnp.where(rows == 22, -low, e)
    side_ref[...] = jnp.zeros_like(side_ref)
    side_ref[0:FEATS, 0:TILE] = depth_rows(s).astype(BF)
    side_ref[0:FEATS, TILE:] = e.astype(BF)


def tile_rows(t):
    return pl.ds(pl.multiple_of(t * TILE, TILE), TILE)


def kernel_sum(p, dz2):
    r = lax.rsqrt(p)
    value = r * (2.0 + dz2 * (r * r))
    return value


def pair_sum(p, half):
    r = lax.rsqrt(p)
    cube = r * (r * r)
    return (r[:, 0:TILE] + r[:, TILE:]) + half * (cube[:, 0:TILE] + cube[:, TILE:])


def prep_kernel(points, elements, lhs):
    tiles = points.shape[1] // TILE

    def group(g, carry):
        for k in range(GROUP):
            t = g * GROUP + k
            o = pl.multiple_of(t * TILE, TILE)
            pt = points[:, pl.ds(o, TILE)]
            re = elements[pl.ds(t, 1), :].astype(F32)
            high = jnp.floor(re * (1.0 / 256.0))
            f = point_features(pt[0:1], pt[1:2], pt[2:3], [high, re - 256.0 * high])
            lhs[pl.ds(o, TILE), :] = f.T.astype(BF)
        return carry

    lax.fori_loop(0, tiles // GROUP, group, 0)


def assemble(count, lhs, out, tab, side, depth, ahead, first_tile):
    tiles = out.shape[0] // TILE

    def start(g, carry):
        for k in range(GROUP):
            t = g * GROUP + k
            a = lhs[tile_rows(first_tile + t), :]
            p = mm(a, tab[0])
            q = mm(a, side[...])
            n = jnp.full((1, TILE), count(first_tile + t), I32).astype(F32)
            half = q[:, 0:TILE] * (q[:, 0:TILE] * 0.5)
            out[tile_rows(t), :] = pair_sum(p, half) + jnp.where(q[:, TILE:] == 0.0, (0.5 * JUMP) * n, 0.0)
            depth[tile_rows(t), :] = half
        return carry

    lax.fori_loop(0, tiles // GROUP, start, 0)

    def fill(slot, t, j):
        tc = jnp.minimum(t, tiles - 1)
        n = count(first_tile + tc)
        index = jnp.where(2 * j + 1 < n, j, PAIRS + j)
        index = jnp.where((t < tiles) & (2 * j < n), index, 2 * PAIRS)
        ahead[slot] = mm(lhs[tile_rows(first_tile + tc), :], tab[index])
        more = 2 * (j + 1) < n
        short = count(first_tile + jnp.minimum(t + 1, tiles - 1)) <= 2
        return tc, jnp.where(more, t, jnp.where(short, t + 2, t + 1)), jnp.where(more, j + 1, 1)

    def fill_all(t, j):
        at = []
        for slot in range(JOBS):
            tc, t, j = fill(slot, t, j)
            at.append(tc)
        return t, j, tuple(at)

    def jobs(state):
        _, t, j, at = state
        for slot in range(JOBS):
            rows = tile_rows(at[slot])
            out[rows, :] = out[rows, :] + pair_sum(ahead[slot], depth[rows, :])
        return (t,) + fill_all(t, j)

    first = jnp.where(count(first_tile) <= 2, 1, 0)
    lax.while_loop(lambda state: state[0] < tiles, jobs, (first,) + fill_all(first, 1))


def own_kernel(counts, lhs, sources, out, tab, side, wide, depth, ahead):
    s = sources[...]
    build_table(s, wide, tab)
    build_side(s, lax.axis_index("col") * TILE, side)
    assemble(lambda t: counts[t], lhs, out, tab, side, depth, ahead, 0)


def rest_kernel(counts, lhs, tab, side, out, depth, ahead, *, first_tile):
    assemble(lambda t: counts[t], lhs, out, tab, side, depth, ahead, first_tile)


def root_kernel(message_scalars, lhs, message, out, tab, side, wide, depth, ahead):
    s = message[0:4]
    build_table(s, wide, tab)
    build_side(s, 0, side)
    assemble(lambda t: message_scalars[4, t].astype(I32), lhs, out, tab, side, depth, ahead, 0)


def pick_kernel(points, pivots, own, root, out):
    tiles = points.shape[1] // TILE
    piv = jnp.broadcast_to(pivots[...], (8, TILE))
    tile = jnp.right_shift(piv, 7) - lax.axis_index("row") * tiles
    lane = jnp.bitwise_and(piv, TILE - 1)
    inside = (tile >= 0) & (tile < tiles)
    found = jnp.zeros((8, TILE), F32)
    for t in range(tiles):
        pt = jnp.concatenate([points[:, t * TILE : (t + 1) * TILE], jnp.zeros((5, TILE), F32)], 0)
        got = jnp.take_along_axis(pt, lane, axis=1, mode="promise_in_bounds")
        found = jnp.where(tile == t, got, found)
    at = jnp.clip(tile, 0, tiles - 1)
    own_counts = jnp.take_along_axis(own[...], at, axis=1, mode="promise_in_bounds")
    root_counts = jnp.take_along_axis(root[...], at, axis=1, mode="promise_in_bounds")
    rows = lax.broadcasted_iota(I32, (8, TILE), 0)
    own_counts = jnp.where(inside, jnp.broadcast_to(own_counts[4:5], (8, TILE)), 0.0)
    root_counts = jnp.where(inside, jnp.broadcast_to(root_counts[4:5], (8, TILE)), 0.0)
    found = jnp.where(rows == 3, own_counts, found)
    out[...] = jnp.where(rows == 4, root_counts, found)


def pivot_block(points, n_row, tab, side, right):
    f = point_features(points[0:1], points[1:2], points[2:3], [n_row])
    a = f.T.astype(BF)
    right[:, 0:TILE] = side[:, 0:TILE]
    q = mm(a, right[...])
    dz = q[:, 0:TILE]
    dz2 = dz * dz
    n = q[:, TILE:]
    total = jnp.zeros((TILE, TILE), F32)
    for j in range(PAIRS):
        p = mm(a, tab[j])
        for k in range(2):
            value = kernel_sum(p[:, k * TILE : (k + 1) * TILE], dz2)
            total = total + (value if 2 * j + k < 2 else jnp.where(n > 2 * j + k, value, 0.0))
    return total / n


def row_bcast(v, j, rows):
    return jnp.broadcast_to(v[j : j + 1, :], (rows, v.shape[1]))


def factor(x_ref, inv_ref, u_ref):
    side = TILE
    sub = lax.broadcasted_iota(I32, (BLOCK, TILE), 0)
    lane = lax.broadcasted_iota(I32, (BLOCK, TILE), 1)
    big = lax.broadcasted_iota(I32, (side, TILE), 0)
    inv_ref[...] = jnp.zeros_like(inv_ref)
    for b in range(side // BLOCK):
        k0 = b * BLOCK
        left = x_ref[k0 : k0 + BLOCK, 0:TILE]
        right = x_ref[k0 : k0 + BLOCK, TILE:]
        cols = [jnp.broadcast_to(left[:, k0 + j : k0 + j + 1], (BLOCK, TILE)) for j in range(BLOCK)]
        upper = jnp.zeros((BLOCK, TILE), F32)
        solved = jnp.zeros((BLOCK, TILE), F32)
        for j in range(BLOCK):
            f = cols[j]
            inv = 1.0 / row_bcast(f, j, BLOCK)
            vcol = jnp.where(sub == j, inv, jnp.where(sub < j, -f * inv, 0.0))
            upper = jnp.where(lane == k0 + j, vcol, upper)
            solved = jnp.where(sub == j, right, solved)
            here = sub == j

            def eliminate(v):
                row = row_bcast(v, j, BLOCK) * inv
                return jnp.where(here, row, v - f * row)

            for jj in range(j + 1, BLOCK):
                cols[jj] = eliminate(cols[jj])
            left = eliminate(left)
            right = eliminate(right)
        u_ref[k0 : k0 + BLOCK, :] = solved
        a = x_ref[:, 0:TILE]

        def rows_at(v):
            parts = []
            if k0:
                parts.append(jnp.zeros((k0, v.shape[1]), F32))
            parts.append(v)
            if k0 + BLOCK < side:
                parts.append(jnp.zeros((side - k0 - BLOCK, v.shape[1]), F32))
            return jnp.concatenate(parts, 0) if len(parts) > 1 else parts[0]

        t = rows_at(jnp.concatenate([left, right], 1))
        a_high, a_low = halves(a)
        prod = mm3(a_high, a_low, t)
        mine = (big >= k0) & (big < k0 + BLOCK)
        x_ref[:, 0:TILE] = jnp.where(mine, t[:, 0:TILE], a - prod[:, 0:TILE])
        x_ref[:, TILE:] = jnp.where(mine, t[:, TILE:], x_ref[:, TILE:] - prod[:, TILE:])
        v = rows_at(upper)
        above = mm3(a_high, a_low, v)
        inv_ref[...] = inv_ref[...] + jnp.where(big < k0, -above, v)


def final_kernel(counts, message, picked, own_tab, own_side, root_tab, root_side, own, rest, root,
                 out_hbm, u_out, right, x, upper, w_ref, ready, out_sems):
    tiles = root.shape[0] // TILE
    early = own.shape[0] // TILE
    is_root = lax.axis_index("col") == 0
    pk = picked[...]
    eye = (lax.broadcasted_iota(I32, (TILE, TILE), 0) == lax.broadcasted_iota(I32, (TILE, TILE), 1))
    right[:, TILE:] = jnp.where(lax.broadcasted_iota(I32, (TILE, TILE), 0) == 24, 1.0, 0.0).astype(BF)
    x[:, 0:TILE] = pivot_block(pk, pk[4:5], root_tab, root_side, right) + jnp.where(eye, JUMP, 0.0)
    x[:, TILE:] = pivot_block(pk, pk[3:4], own_tab, own_side, right) + jnp.where(eye & is_root, JUMP, 0.0)
    factor(x, upper, u_out)
    w = jnp.where(is_root, upper[...], -x[:, TILE:])
    wh = w.astype(BF)
    wl = (w - wh.astype(F32)).astype(BF)
    w_ref[0:TILE, :] = wh
    w_ref[TILE : 2 * TILE, :] = wh
    w_ref[2 * TILE :, :] = wl
    keep = jnp.where(is_root, 0.0, 2.0)

    def out_copy(g):
        rows = pl.ds(pl.multiple_of(g * (GROUP * TILE), TILE), GROUP * TILE)
        return pltpu.make_async_copy(ready.at[rows, :], out_hbm.at[rows, :], out_sems.at[g])

    def part(block, first):
        def group(g, carry):
            for k in range(GROUP):
                at = g * GROUP + k
                t = first + at
                rows = tile_rows(t)
                n0 = jnp.full((1, TILE), message[4, t], F32)
                nc = jnp.full((1, TILE), counts[t], I32).astype(F32)
                h, l = halves(root[rows, :] * (2.0 / n0))
                prod = mm(jnp.concatenate([h, l], 1), w_ref[0 : 2 * TILE, :]) + mm(h, w_ref[2 * TILE :, :])
                ready[rows, :] = block[tile_rows(at), :] * (keep / nc) + prod
            out_copy(first // GROUP + g).start()
            return carry

        lax.fori_loop(0, block.shape[0] // TILE // GROUP, group, 0)

    part(own, 0)
    part(rest, early)

    def finish(g, carry):
        out_copy(g).wait()
        return carry

    lax.fori_loop(0, tiles // GROUP, finish, 0)


def vmem():
    return pl.BlockSpec(memory_space=pltpu.VMEM)


def smem():
    return pl.BlockSpec(memory_space=pltpu.SMEM)


def hbm():
    return pl.BlockSpec(memory_space=pl.ANY)


def numbered(send, steps):
    parts = []
    for k in steps:
        parts.append(send(k))
    return parts


def limit(mib):
    return pltpu.CompilerParams(vmem_limit_bytes=mib * 1024 * 1024)


def steps(colloc_points, sources, counts, row_element, pivots):
    local_rows = colloc_points.shape[1]
    tiles = local_rows // TILE
    early = tiles // 2
    own_counts = counts.reshape(tiles)
    col = lax.axis_index("col")
    table = jax.ShapeDtypeStruct((2 * PAIRS + 1, TILE, 2 * TILE), BF)
    aside = jax.ShapeDtypeStruct((TILE, 2 * TILE), BF)

    def part(count):
        return jax.ShapeDtypeStruct((count * TILE, TILE), F32)

    wide = pltpu.VMEM((QUAD_MAX * FEATS, TILE), F32)

    def work(count):
        return [pltpu.VMEM((count * TILE, TILE), F32), pltpu.VMEM((JOBS, TILE, 2 * TILE), F32)]

    count_row = jnp.pad(own_counts.astype(F32)[None, :], ((0, 3), (0, TILE - tiles)))
    message = jnp.concatenate([sources, count_row], 0)
    got = numbered(lambda k: lax.ppermute(message, "col", [(0, k)]), (2, 1, 3))
    y_part = jnp.where(col == 0, message, got[0] + got[1] + got[2])
    got = numbered(lambda k: lax.ppermute(y_part, "col", [(i, i + k) for i in range(4)]), (8, 4, 12))
    root_message = jnp.where(col < 4, y_part, got[0] + got[1] + got[2])
    lhs = pl.pallas_call(
        prep_kernel,
        out_shape=jax.ShapeDtypeStruct((local_rows, TILE), BF),
        in_specs=[vmem(), vmem()],
        out_specs=vmem(),
        compiler_params=limit(8),
        name="prep",
    )(colloc_points, row_element.reshape(tiles, TILE))
    own_sum, own_tab, own_side = pl.pallas_call(
        own_kernel,
        out_shape=(part(early), table, aside),
        in_specs=[smem(), vmem(), vmem()],
        out_specs=(vmem(), vmem(), vmem()),
        scratch_shapes=[wide] + work(early),
        compiler_params=limit(12),
        name="own",
    )(own_counts, lhs, sources)
    picked = pl.pallas_call(
        pick_kernel,
        out_shape=jax.ShapeDtypeStruct((8, TILE), F32),
        in_specs=[vmem()] * 4,
        out_specs=vmem(),
        compiler_params=limit(4),
        name="pick",
    )(colloc_points, pivots.reshape(1, TILE), message, root_message)
    picked = picked + lax.ppermute(picked, "row", [(i, i ^ 1) for i in range(8)])
    got = numbered(lambda k: lax.ppermute(picked, "row", [(i, i ^ k) for i in range(8)]), (4, 2, 6))
    picked = picked + got[0] + got[1] + got[2]
    rest_sum = pl.pallas_call(
        functools.partial(rest_kernel, first_tile=early),
        out_shape=part(tiles - early),
        in_specs=[smem(), vmem(), vmem(), vmem()],
        out_specs=vmem(),
        scratch_shapes=work(tiles - early),
        compiler_params=limit(12),
        name="rest",
    )(own_counts, lhs, own_tab, own_side)
    root_sum, root_tab, root_side = pl.pallas_call(
        root_kernel,
        out_shape=(part(tiles), table, aside),
        in_specs=[smem(), vmem(), vmem()],
        out_specs=(vmem(), vmem(), vmem()),
        scratch_shapes=[wide] + work(tiles),
        compiler_params=limit(18),
        name="root",
    )(root_message, lhs, root_message)
    return pl.pallas_call(
        final_kernel,
        out_shape=(
            jax.ShapeDtypeStruct((local_rows, TILE), F32),
            jax.ShapeDtypeStruct((TILE, TILE), F32),
        ),
        in_specs=[smem(), smem()] + [vmem()] * 8,
        out_specs=(hbm(), vmem()),
        scratch_shapes=[
            pltpu.VMEM((TILE, 2 * TILE), BF),
            pltpu.VMEM((TILE, 2 * TILE), F32),
            pltpu.VMEM((TILE, TILE), F32),
            pltpu.VMEM((3 * TILE, TILE), BF),
            pltpu.VMEM((local_rows, TILE), F32),
            pltpu.SemaphoreType.DMA((tiles // GROUP,)),
        ],
        compiler_params=limit(16),
        name="final",
    )(own_counts, root_message, picked, own_tab, own_side, root_tab, root_side, own_sum, rest_sum, root_sum)


def solution(mesh):
    placed = (P(None, "row"), P(None, "col"), P("row", "col"), P("row"), P())
    return jax.shard_map(
        steps,
        mesh=mesh,
        in_specs=placed,
        out_specs=(P("row", "col"), P(None, "col")),
        check_vma=False,
    )
```

profile of v0, /device:TPU:27, one launch (start us, length us, event | category | flops | bytes accessed | tf_op | source)
XLA Modules:
  0.0 64.0 jit_solution(13776923147101708145)
XLA Ops:
  0.6 0.0 copy-start.4
  0.6 0.0 copy-start.3
  0.7 0.7 %convert_bitcast_fusion = f32[1,60]{1,0:T(1,128)S(1)} fusion(s32[60,1]{0,1:T(1,128)} %param.7), kind=kLoop, calls=%fused_computation.5 | loop fusion | flops 60 | bytes 480 | tf_op jit(solution)/shard_map/convert_element_type | solution.py:417
  1.4 0.7 %select_maximum_fusion.own = f32[8,128]{1,0:T(8,128)S(1)} fusion(f32[1,60]{1,0:T(1,128)S(1)} %convert_bitcast_fusion, f32[4,128]{1,0:T(4,128)} %sources.1), kind=kLoop, calls=%fused_computation | loop fusion | flops 3072 | bytes 6384 | tf_op jit(solution)/shard_map/concatenate | solution.py:418
  2.1 0.6 %collective-permute-start.2 = (f32[8,128]{1,0:T(8,128)S(1)}, f32[8,128]{1,0:T(8,128)S(1)}, u32[]{:S(2)}, u32[]{:S(2)}) collective-permute-start(f32[8,128]{1,0:T(8,128)S(1)} %select_maximum_fusion.own), channel_id=1, source_target_pairs={{0,3},{16,19},{32,35},{48,51},{64,67},{80,83},{96,99},{112,115}} | collective-permute-start | bytes 12296 | tf_op jit(solution)/shard_map/ppermute | solution.py:419
  2.7 0.7 %collective-permute-start.1 = (f32[8,128]{1,0:T(8,128)S(1)}, f32[8,128]{1,0:T(8,128)S(1)}, u32[]{:S(2)}, u32[]{:S(2)}) collective-permute-start(f32[8,128]{1,0:T(8,128)S(1)} %select_maximum_fusion.own), channel_id=1, source_target_pairs={{0,1},{16,17},{32,33},{48,49},{64,65},{80,81},{96,97},{112,113}} | collective-permute-start | bytes 12296 | tf_op jit(solution)/shard_map/ppermute | solution.py:419
  3.4 0.7 %collective-permute-start = (f32[8,128]{1,0:T(8,128)S(1)}, f32[8,128]{1,0:T(8,128)S(1)}, u32[]{:S(2)}, u32[]{:S(2)}) collective-permute-start(f32[8,128]{1,0:T(8,128)S(1)} %select_maximum_fusion.own), channel_id=1, source_target_pairs={{0,2},{16,18},{32,34},{48,50},{64,66},{80,82},{96,98},{112,114}} | collective-permute-start | bytes 12296 | tf_op jit(solution)/shard_map/ppermute | solution.py:419
  4.1 0.0 collective-permute-done.2
  4.1 0.0 collective-permute-done.1
  4.1 0.0 collective-permute-done
  4.1 0.7 %add_select_fusion.1 = f32[8,128]{1,0:T(8,128)S(1)} fusion(f32[8,128]{1,0:T(8,128)S(1)} %collective-permute-done.2, f32[8,128]{1,0:T(8,128)S(1)} %collective-permute-done, f32[8,128]{1,0:T(8,128)S(1)} %collective-permute-done.1, pred[]{:T(512)S(6)} %eq.3, f32[1,60]{1,0:T(1,128)S(1)} %convert_bitcast_fusion, f32[4,128]{1,0:T(4,128)} %sources.1), kind=kLoop, calls=%fused_computation.4 | loop fusion | flops 6144 | bytes 18673 | tf_op jit(solution)/shard_map/jit(_where)/select_n | solution.py:420
  4.8 0.6 %collective-permute-start.5 = (f32[8,128]{1,0:T(8,128)S(1)}, f32[8,128]{1,0:T(8,128)S(1)}, u32[]{:S(2)}, u32[]{:S(2)}) collective-permute-start(f32[8,128]{1,0:T(8,128)S(1)} %add_select_fusion.1), channel_id=1, source_target_pairs={{0,12},{1,13},{2,14},{3,15},{16,28},{17,29},{18,30},{19,31},{32,44... | collective-permute-start | bytes 12296 | tf_op jit(solution)/shard_map/ppermute | solution.py:421
  5.4 1.3 %collective-permute-start.4 = (f32[8,128]{1,0:T(8,128)S(1)}, f32[8,128]{1,0:T(8,128)S(1)}, u32[]{:S(2)}, u32[]{:S(2)}) collective-permute-start(f32[8,128]{1,0:T(8,128)S(1)} %add_select_fusion.1), channel_id=1, source_target_pairs={{0,4},{1,5},{2,6},{3,7},{16,20},{17,21},{18,22},{19,23},{32,36},{3... | collective-permute-start | bytes 12296 | tf_op jit(solution)/shard_map/ppermute | solution.py:421
  6.7 0.7 %collective-permute-start.3 = (f32[8,128]{1,0:T(8,128)S(1)}, f32[8,128]{1,0:T(8,128)S(1)}, u32[]{:S(2)}, u32[]{:S(2)}) collective-permute-start(f32[8,128]{1,0:T(8,128)S(1)} %add_select_fusion.1), channel_id=1, source_target_pairs={{0,8},{1,9},{2,10},{3,11},{16,24},{17,25},{18,26},{19,27},{32,40},... | collective-permute-start | bytes 12296 | tf_op jit(solution)/shard_map/ppermute | solution.py:421
  7.4 0.0 collective-permute-done.5
  7.4 4.7 %collective-permute-done.4 = f32[8,128]{1,0:T(8,128)S(1)} collective-permute-done((f32[8,128]{1,0:T(8,128)S(1)}, f32[8,128]{1,0:T(8,128)S(1)}, u32[]{:S(2)}, u32[]{:S(2)}) %collective-permute-start.4) | collective-permute-done | bytes 4128 | tf_op jit(solution)/shard_map/ppermute | solution.py:421
  12.1 0.0 collective-permute-done.3
  12.1 0.0 copy-start
  12.1 0.9 %copy-done = f32[3,7680]{1,0:T(4,128)S(1)} copy-done((f32[3,7680]{1,0:T(4,128)S(1)}, f32[3,7680]{1,0:T(4,128)}, u32[]{:S(2)}) %copy-start) | copy-done | bytes 92184
  13.0 0.0 copy-start.5
  13.0 0.7 %copy-done.5 = s32[128]{0:T(128)S(1)} copy-done((s32[128]{0:T(128)S(1)}, s32[128]{0:T(128)}, u32[]{:S(2)}) %copy-start.5) | copy-done | bytes 536
  13.7 0.1 pick.1
  13.8 2.8 %collective-permute-start.6 = (f32[8,128]{1,0:T(8,128)S(1)}, f32[8,128]{1,0:T(8,128)S(1)}, u32[]{:S(2)}, u32[]{:S(2)}) collective-permute-start(f32[8,128]{1,0:T(8,128)S(1)} %pick.1), channel_id=1, source_target_pairs={{0,16},{16,0},{32,48},{48,32},{64,80},{80,64},{96,112},{112,96},{1... | collective-permute-start | bytes 12296 | tf_op jit(solution)/shard_map/ppermute | solution.py:448
  16.6 0.8 %collective-permute-done.6 = f32[8,128]{1,0:T(8,128)S(1)} collective-permute-done((f32[8,128]{1,0:T(8,128)S(1)}, f32[8,128]{1,0:T(8,128)S(1)}, u32[]{:S(2)}, u32[]{:S(2)}) %collective-permute-start.6) | collective-permute-done | bytes 4128 | tf_op jit(solution)/shard_map/ppermute | solution.py:448
  17.4 3.8 %collective-permute-start.9 = (f32[8,128]{1,0:T(8,128)S(1)}, f32[8,128]{1,0:T(8,128)S(1)}, u32[]{:S(2)}, u32[]{:S(2)}) collective-permute-start(f32[8,128]{1,0:T(8,128)S(1)} %add.30), channel_id=1, source_target_pairs={{0,96},{16,112},{32,64},{48,80},{64,32},{80,48},{96,0},{112,16},{1... | collective-permute-start | bytes 12296 | tf_op jit(solution)/shard_map/ppermute | solution.py:449
  21.2 0.0 collective-permute-start.8
  21.2 1.2 %collective-permute-start.7 = (f32[8,128]{1,0:T(8,128)S(1)}, f32[8,128]{1,0:T(8,128)S(1)}, u32[]{:S(2)}, u32[]{:S(2)}) collective-permute-start(f32[8,128]{1,0:T(8,128)S(1)} %add.30), channel_id=1, source_target_pairs={{0,64},{16,80},{32,96},{48,112},{64,0},{80,16},{96,32},{112,48},{1... | collective-permute-start | bytes 12296 | tf_op jit(solution)/shard_map/ppermute | solution.py:449
  22.4 0.0 copy-start.1
  22.4 0.9 %copy-done.1 = f32[3,7680]{1,0:T(4,128)S(1)} copy-done((f32[3,7680]{1,0:T(4,128)S(1)}, f32[3,7680]{1,0:T(4,128)}, u32[]{:S(2)}) %copy-start.1) | copy-done | bytes 92184
  23.3 0.0 copy-start.2
  23.3 0.8 %copy-done.2 = s32[7680]{0:T(1024)S(1)} copy-done((s32[7680]{0:T(1024)S(1)}, s32[7680]{0:T(1024)}, u32[]{:S(2)}) %copy-start.2) | copy-done | bytes 30744
  24.0 1.3 %prep.1.lhs = bf16[7680,128]{1,0:T(8,128)(2,1)S(1)} custom-call(f32[3,7680]{1,0:T(4,128)S(1)} %copy-done.1, s32[60,128]{1,0:T(8,128)S(1)} %bitcast.5), custom_call_target="tpu_custom_call" | custom-call | tf_op jit(solution)/shard_map/prep/pallas_call | solution.py:423
  25.4 0.0 copy-done.4
  25.4 0.0 copy-done.3
  25.4 10.5 %own.1 = (f32[3840,128]{1,0:T(8,128)S(1)}, bf16[17,128,256]{2,1,0:T(8,128)(2,1)S(1)}, bf16[128,256]{1,0:T(8,128)(2,1)S(1)}) custom-call(s32[60]{0:T(128)S(1)} %bitcast.6, bf16[7680,128]{1,0:T(8,128)(2,1)S(1)} %prep.1.lhs, f32[4,128]{1,0:T(4,128)S(1)} %copy-done.3), custom_call_target="tpu_custom_call" | custom-call | tf_op jit(solution)/shard_map/own/pallas_call | solution.py:431
  35.9 10.7 %rest.1 = f32[3840,128]{1,0:T(8,128)S(1)} custom-call(s32[60]{0:T(128)S(1)} %bitcast.7, bf16[7680,128]{1,0:T(8,128)(2,1)S(1)} %prep.1.lhs, bf16[17,128,256]{2,1,0:T(8,128)(2,1)S(1)} %get-tuple-element.8.tab.own_tab, bf16[128,256]{1,0:T(8,128)(2,1)S(1)} %get-tuple-element.9.side.own_side), custom_call_target="tpu_custom_call" | custom-call | tf_op jit(solution)/shard_map/rest/pallas_call | solution.py:451
  46.6 7.8 %root.1 = (f32[7680,128]{1,0:T(8,128)S(1)}, bf16[17,128,256]{2,1,0:T(8,128)(2,1)S(1)}, bf16[128,256]{1,0:T(8,128)(2,1)S(1)}) custom-call(f32[8,128]{1,0:T(8,128)S(1)} %add_select_fusion.root.message_scalars.message, bf16[7680,128]{1,0:T(8,128)(2,1)S(1)} %prep.1.lhs, f32[8,128]{1,0:T(8,128)S(1)} %add_select_fusion.root.message_scalars.message), custom_call_target="tpu_custom_call" | custom-call | tf_op jit(solution)/shard_map/root/pallas_call | solution.py:460
  54.5 0.0 collective-permute-done.9
  54.5 0.0 collective-permute-done.8
  54.5 0.0 collective-permute-done.7
  54.5 9.5 %final.1 = (f32[7680,128]{1,0:T(8,128)}, f32[128,128]{1,0:T(8,128)}) custom-call(s32[60]{0:T(128)S(1)} %bitcast.8, f32[8,128]{1,0:T(8,128)S(1)} %add_select_fusion.root.message_scalars.message, f32[8,128]{1,0:T(8,128)S(1)} %add_add_fusion.picked, bf16[17,128,256]{2,1,0:T(8,128)(2,1)S(1)} %get-tuple-element.8.tab.own_tab, ...), custom_call_target="tpu_custom_call" | custom-call | tf_op jit(solution)/shard_map/final/pallas_call | solution.py:469
  (3 shorter events, 0.0 us)
Async XLA Ops:
  0.6 24.8 %copy-start.4 = (s32[60,1]{0,1:T(1,128)S(1)}, s32[60,1]{0,1:T(1,128)}, u32[]{:S(2)}) copy-start(s32[60,1]{0,1:T(1,128)} %param.7) | copy-start | bytes 724
  0.6 24.8 %copy-start.3 = (f32[4,128]{1,0:T(4,128)S(1)}, f32[4,128]{1,0:T(4,128)}, u32[]{:S(2)}) copy-start(f32[4,128]{1,0:T(4,128)} %sources.1) | copy-start | bytes 6148
  2.1 2.0 %collective-permute-start.2 = (f32[8,128]{1,0:T(8,128)S(1)}, f32[8,128]{1,0:T(8,128)S(1)}, u32[]{:S(2)}, u32[]{:S(2)}) collective-permute-start(f32[8,128]{1,0:T(8,128)S(1)} %select_maximum_fusion.own), channel_id=1, source_target_pairs={{0,3},{16,19},{32,35},{48,51},{64,67},{80,83},{96,99},{112,115}} | collective-permute-start | bytes 12296 | tf_op jit(solution)/shard_map/ppermute | solution.py:419
  2.7 1.4 %collective-permute-start.1 = (f32[8,128]{1,0:T(8,128)S(1)}, f32[8,128]{1,0:T(8,128)S(1)}, u32[]{:S(2)}, u32[]{:S(2)}) collective-permute-start(f32[8,128]{1,0:T(8,128)S(1)} %select_maximum_fusion.own), channel_id=1, source_target_pairs={{0,1},{16,17},{32,33},{48,49},{64,65},{80,81},{96,97},{112,113}} | collective-permute-start | bytes 12296 | tf_op jit(solution)/shard_map/ppermute | solution.py:419
  3.4 0.7 %collective-permute-start = (f32[8,128]{1,0:T(8,128)S(1)}, f32[8,128]{1,0:T(8,128)S(1)}, u32[]{:S(2)}, u32[]{:S(2)}) collective-permute-start(f32[8,128]{1,0:T(8,128)S(1)} %select_maximum_fusion.own), channel_id=1, source_target_pairs={{0,2},{16,18},{32,34},{48,50},{64,66},{80,82},{96,98},{112,114}} | collective-permute-start | bytes 12296 | tf_op jit(solution)/shard_map/ppermute | solution.py:419
  4.8 2.6 %collective-permute-start.5 = (f32[8,128]{1,0:T(8,128)S(1)}, f32[8,128]{1,0:T(8,128)S(1)}, u32[]{:S(2)}, u32[]{:S(2)}) collective-permute-start(f32[8,128]{1,0:T(8,128)S(1)} %add_select_fusion.1), channel_id=1, source_target_pairs={{0,12},{1,13},{2,14},{3,15},{16,28},{17,29},{18,30},{19,31},{32,44... | collective-permute-start | bytes 12296 | tf_op jit(solution)/shard_map/ppermute | solution.py:421
  5.4 6.7 %collective-permute-start.4 = (f32[8,128]{1,0:T(8,128)S(1)}, f32[8,128]{1,0:T(8,128)S(1)}, u32[]{:S(2)}, u32[]{:S(2)}) collective-permute-start(f32[8,128]{1,0:T(8,128)S(1)} %add_select_fusion.1), channel_id=1, source_target_pairs={{0,4},{1,5},{2,6},{3,7},{16,20},{17,21},{18,22},{19,23},{32,36},{3... | collective-permute-start | bytes 12296 | tf_op jit(solution)/shard_map/ppermute | solution.py:421
  6.7 5.4 %collective-permute-start.3 = (f32[8,128]{1,0:T(8,128)S(1)}, f32[8,128]{1,0:T(8,128)S(1)}, u32[]{:S(2)}, u32[]{:S(2)}) collective-permute-start(f32[8,128]{1,0:T(8,128)S(1)} %add_select_fusion.1), channel_id=1, source_target_pairs={{0,8},{1,9},{2,10},{3,11},{16,24},{17,25},{18,26},{19,27},{32,40},... | collective-permute-start | bytes 12296 | tf_op jit(solution)/shard_map/ppermute | solution.py:421
  12.1 0.9 %copy-start = (f32[3,7680]{1,0:T(4,128)S(1)}, f32[3,7680]{1,0:T(4,128)}, u32[]{:S(2)}) copy-start(f32[3,7680]{1,0:T(4,128)} %points.3) | copy-start | bytes 276484
  13.0 0.7 %copy-start.5 = (s32[128]{0:T(128)S(1)}, s32[128]{0:T(128)}, u32[]{:S(2)}) copy-start(s32[128]{0:T(128)} %param.9) | copy-start | bytes 1540
  13.8 3.6 %collective-permute-start.6 = (f32[8,128]{1,0:T(8,128)S(1)}, f32[8,128]{1,0:T(8,128)S(1)}, u32[]{:S(2)}, u32[]{:S(2)}) collective-permute-start(f32[8,128]{1,0:T(8,128)S(1)} %pick.1), channel_id=1, source_target_pairs={{0,16},{16,0},{32,48},{48,32},{64,80},{80,64},{96,112},{112,96},{1... | collective-permute-start | bytes 12296 | tf_op jit(solution)/shard_map/ppermute | solution.py:448
  17.4 37.0 %collective-permute-start.9 = (f32[8,128]{1,0:T(8,128)S(1)}, f32[8,128]{1,0:T(8,128)S(1)}, u32[]{:S(2)}, u32[]{:S(2)}) collective-permute-start(f32[8,128]{1,0:T(8,128)S(1)} %add.30), channel_id=1, source_target_pairs={{0,96},{16,112},{32,64},{48,80},{64,32},{80,48},{96,0},{112,16},{1... | collective-permute-start | bytes 12296 | tf_op jit(solution)/shard_map/ppermute | solution.py:449
  21.2 33.3 %collective-permute-start.8 = (f32[8,128]{1,0:T(8,128)S(1)}, f32[8,128]{1,0:T(8,128)S(1)}, u32[]{:S(2)}, u32[]{:S(2)}) collective-permute-start(f32[8,128]{1,0:T(8,128)S(1)} %add.30), channel_id=1, source_target_pairs={{0,32},{16,48},{32,0},{48,16},{64,96},{80,112},{96,64},{112,80},{1... | collective-permute-start | bytes 12296 | tf_op jit(solution)/shard_map/ppermute | solution.py:449
  21.2 33.3 %collective-permute-start.7 = (f32[8,128]{1,0:T(8,128)S(1)}, f32[8,128]{1,0:T(8,128)S(1)}, u32[]{:S(2)}, u32[]{:S(2)}) collective-permute-start(f32[8,128]{1,0:T(8,128)S(1)} %add.30), channel_id=1, source_target_pairs={{0,64},{16,80},{32,96},{48,112},{64,0},{80,16},{96,32},{112,48},{1... | collective-permute-start | bytes 12296 | tf_op jit(solution)/shard_map/ppermute | solution.py:449
  22.4 0.9 %copy-start.1 = (f32[3,7680]{1,0:T(4,128)S(1)}, f32[3,7680]{1,0:T(4,128)}, u32[]{:S(2)}) copy-start(f32[3,7680]{1,0:T(4,128)} %points.3) | copy-start | bytes 276484
  23.3 0.8 %copy-start.2 = (s32[7680]{0:T(1024)S(1)}, s32[7680]{0:T(1024)}, u32[]{:S(2)}) copy-start(s32[7680]{0:T(1024)} %param.8) | copy-start | bytes 92164
where the time goes:
time: 64.4 us; the launch traced here: 64 us
  Pallas kernels  40 us (62%)
  starting transfers between devices  12.3 us (19%)
  waiting for transfers between devices  5.54 us (9%)
  local copies, waits for them, and re-layouts  3.22 us (5%)
  other arithmetic  2.11 us (3%)
  between operations  0.83 us (1%)
    pallas_call x1, Pallas kernels, steps(): pl.pallas_call(functools.partial(rest_kernel, first_tile=early), out_shap...  10.7 us
    pallas_call x1, Pallas kernels, steps(): pl.pallas_call(own_kernel, out_shape=(part(early), table, aside), in_spec...  10.5 us
    pallas_call x1, Pallas kernels, steps(): pl.pallas_call(final_kernel, out_shape=(jax.ShapeDtypeStruct((local_rows,...  9.47 us
    pallas_call x1, Pallas kernels, steps(): pl.pallas_call(root_kernel, out_shape=(part(tiles), table, aside), in_spe...  7.85 us
    ppermute x3, starting transfers between devices, steps(): lax.ppermute(picked, 'row', [(i, i ^ k) for i in range(8)])  4.94 us
    ppermute x3, waiting for transfers between devices, steps(): lax.ppermute(y_part, 'col', [(i, i + k) for i in range(4)])  4.7 us
    unnamed x12, local copies, waits for them, and re-layouts  3.22 us
    ppermute x1, starting transfers between devices, steps(): lax.ppermute(picked, 'row', [(i, i ^ 1) for i in range(8)])  2.77 us
  transfers between devices with their start and end apart: 10, of which 2 were waited for; matrix products, arithmetic and copies ran while one was open for 0% of the time, Pallas kernels for 47%

commit v1 on v0

v1 whole, which is shorter than its diff:
```python
import functools

import jax
import jax.numpy as jnp
import numpy as np
from jax import lax
from jax.experimental import pallas as pl
from jax.experimental.pallas import tpu as pltpu
from jax.sharding import PartitionSpec as P


F32 = jnp.float32
BF = jnp.bfloat16
I32 = jnp.int32

TILE = 128
QUAD_MAX = 16
PAIRS = QUAD_MAX // 2
FEATS = 32
JUMP = 512.0
BLOCK = 16
GROUP = 10
JOBS = 8
DEPTH = 256
WAYS = 6


def split3(v):
    high = v.astype(BF).astype(F32)
    rest = v - high
    mid = rest.astype(BF).astype(F32)
    low = (rest - mid).astype(BF).astype(F32)
    return high, mid, low


def mm(a, b):
    return jnp.dot(a, b, preferred_element_type=F32)


def halves(v):
    high = v.astype(BF)
    return high, (v - high.astype(F32)).astype(BF)


def point_features(x, y, z, extra):
    xs = x - 0.5
    ys = y - 0.5
    rows = []
    for v in (xs, ys, z):
        h, m, l = split3(v)
        rows += [h, h, m, m, h, l]
    rows += list(split3(xs * xs + ys * ys + z * z))
    one = jnp.ones_like(x)
    rows += [one, one, one]
    rows += extra
    zero = jnp.zeros_like(x)
    rows += [zero] * (FEATS - len(rows))
    rows = jnp.concatenate(rows, 0)
    return jnp.concatenate([rows, jnp.zeros((TILE - FEATS, TILE), F32)], 0)


def quad_offsets():
    numbers = np.arange(QUAD_MAX).astype(np.float32)
    radius = np.float32(4.0) * np.sqrt((numbers + np.float32(0.5)) / np.float32(QUAD_MAX))
    angles = np.float32(2.39996323) * numbers
    return radius * np.cos(angles), radius * np.sin(angles)


def build_table(s, wide_ref, tab_ref):
    off_x, off_y = quad_offsets()
    numbers = lax.broadcasted_iota(I32, (QUAD_MAX, TILE), 0)
    ox = jnp.zeros((QUAD_MAX, TILE), F32)
    oy = ox
    for q in range(QUAD_MAX):
        ox = jnp.where(numbers == q, float(off_x[q]), ox)
        oy = jnp.where(numbers == q, float(off_y[q]), oy)
    sx, sy, sz, size = [jnp.broadcast_to(s[i : i + 1], (QUAD_MAX, TILE)) for i in range(4)]
    ux = (sx + size * ox) - 0.5
    uy = (sy + size * oy) - 0.5
    norm = ux * ux + uy * uy + sz * sz + size * size
    wide_ref[...] = jnp.zeros_like(wide_ref)

    def put(f, v):
        wide_ref[pl.ds(f, QUAD_MAX, stride=FEATS), :] = v

    for base, u in ((0, -2.0 * ux), (6, -2.0 * uy), (12, -2.0 * sz)):
        uh, um, ul = split3(u)
        for k, v in enumerate((uh, um, uh, um, ul, uh)):
            put(base + k, v)
    one = jnp.ones((QUAD_MAX, TILE), F32)
    for k in range(3):
        put(18 + k, one)
    for k, v in enumerate(split3(norm)):
        put(21 + k, v)
    rows = lax.broadcasted_iota(I32, (FEATS, TILE), 0)
    far = jnp.where(rows == 21, 1e30, 0.0).astype(BF)
    for q in range(QUAD_MAX):
        block = wide_ref[pl.ds(FEATS * q, FEATS), :].astype(BF)
        j = q // 2
        if q % 2 == 0:
            tab_ref[j, 0:FEATS, 0:TILE] = block
            tab_ref[PAIRS + j, 0:FEATS, 0:TILE] = block
            tab_ref[PAIRS + j, 0:FEATS, TILE:] = far
        else:
            tab_ref[j, 0:FEATS, TILE:] = block
    tab_ref[2 * PAIRS, 0:FEATS, 0:TILE] = far
    tab_ref[2 * PAIRS, 0:FEATS, TILE:] = far


def depth_rows(s):
    rows = lax.broadcasted_iota(I32, (FEATS, TILE), 0)
    zh, zm, zl = split3(jnp.broadcast_to(s[2:3], (FEATS, TILE)))
    dz = jnp.where((rows == 12) | (rows == 14) | (rows == 17), 1.0, 0.0)
    dz = jnp.where(rows == 21, -zh, dz)
    dz = jnp.where(rows == 22, -zm, dz)
    return jnp.where(rows == 23, -zl, dz)


def build_side(s, first_col, side_ref):
    rows = lax.broadcasted_iota(I32, (FEATS, TILE), 0)
    ids = (lax.broadcasted_iota(I32, (FEATS, TILE), 1) + first_col).astype(F32)
    high = jnp.floor(ids * (1.0 / 256.0))
    low = ids - 256.0 * high
    e = jnp.where(rows == 24, 256.0, 0.0)
    e = jnp.where(rows == 25, 1.0, e)
    e = jnp.where(rows == 21, -256.0 * high, e)
    e = jnp.where(rows == 22, -low, e)
    side_ref[0:FEATS, 0:TILE] = depth_rows(s).astype(BF)
    side_ref[0:FEATS, TILE:] = e.astype(BF)


def tile_rows(t):
    return pl.ds(pl.multiple_of(t * TILE, TILE), TILE)


def kernel_sum(p, dz2):
    r = lax.rsqrt(p)
    value = r * (2.0 + dz2 * (r * r))
    return value


def pair_sum(p, half):
    r = lax.rsqrt(p)
    cube = r * (r * r)
    return (r[:, 0:TILE] + r[:, TILE:]) + half * (cube[:, 0:TILE] + cube[:, TILE:])


def build_lhs(points, elements, lhs):
    tiles = points.shape[1] // TILE

    def group(g, carry):
        for k in range(GROUP):
            t = g * GROUP + k
            o = pl.multiple_of(t * TILE, TILE)
            pt = points[:, pl.ds(o, TILE)]
            re = elements[pl.ds(t, 1), :].astype(F32)
            high = jnp.floor(re * (1.0 / 256.0))
            f = point_features(pt[0:1], pt[1:2], pt[2:3], [high, re - 256.0 * high])
            lhs[pl.ds(o, TILE), :] = f.T.astype(BF)
        return carry

    lax.fori_loop(0, tiles // GROUP, group, 0)


def pack_kernel(sources_hbm, counts_hbm, out, counts, sems):
    loads = [
        pltpu.make_async_copy(sources_hbm, out.at[pl.ds(0, 4), :], sems.at[0]),
        pltpu.make_async_copy(counts_hbm, counts, sems.at[1]),
    ]
    for load in loads:
        load.start()
    out[4:, :] = jnp.zeros((4, TILE), F32)
    for load in loads:
        load.wait()
    out[4:5, 0 : counts.shape[1]] = counts[...].astype(F32)


def wide_lhs(a):
    return jnp.concatenate([a, jnp.zeros((a.shape[0], DEPTH - a.shape[1]), BF)], 1)


def tall(b, rows):
    return jnp.concatenate([b, jnp.zeros((rows - b.shape[0], b.shape[1]), BF)], 0)


def send(acc, a, b, slot):
    pltpu.matmul_push_rhs(tall(b, DEPTH), slot // 2 % 2, slot % 2)
    pltpu.matmul_acc_lhs(acc, wide_lhs(a), load_staged_rhs=slot // 2 % 2)


def assemble(count, lhs, out, tab, side, depth, first_tile, *accs):
    tiles = out.shape[0] // TILE

    def begin(slot, t):
        a = lhs[tile_rows(first_tile + jnp.minimum(t, tiles - 1)), :]
        send(accs[2 * slot], a, tab[0], 2 * slot)
        send(accs[2 * slot + 1], a, side[...], 2 * slot + 1)

    def finish(slot, t):
        p = pltpu.matmul_pop(accs[2 * slot])
        q = pltpu.matmul_pop(accs[2 * slot + 1])
        n = jnp.full((1, TILE), count(first_tile + t), I32).astype(F32)
        half = q[:, 0:TILE] * (q[:, 0:TILE] * 0.5)
        out[tile_rows(t), :] = pair_sum(p, half) + jnp.where(q[:, TILE:] == 0.0, (0.5 * JUMP) * n, 0.0)
        depth[tile_rows(t), :] = half

    ways = JOBS // 2
    for slot in range(ways):
        begin(slot, slot)

    def start(g, carry):
        for slot in range(ways):
            t = g * ways + slot
            finish(slot, jnp.minimum(t, tiles - 1))
            begin(slot, t + ways)
        return carry

    lax.fori_loop(0, (tiles + ways - 1) // ways, start, 0)
    for acc in accs:
        pltpu.matmul_pop(acc)

    def fill(slot, t, j):
        tc = jnp.minimum(t, tiles - 1)
        n = count(first_tile + tc)
        index = jnp.where(2 * j + 1 < n, j, PAIRS + j)
        index = jnp.where((t < tiles) & (2 * j < n), index, 2 * PAIRS)
        send(accs[slot], lhs[tile_rows(first_tile + tc), :], tab[index], slot)
        more = 2 * (j + 1) < n
        short = count(first_tile + jnp.minimum(t + 1, tiles - 1)) <= 2
        return tc, jnp.where(more, t, jnp.where(short, t + 2, t + 1)), jnp.where(more, j + 1, 1)

    def jobs(state):
        _, t, j, at = state
        upcoming = []
        at_start = t
        for slot in range(JOBS):
            rows = tile_rows(at[slot])
            p = pltpu.matmul_pop(accs[slot])
            out[rows, :] = out[rows, :] + pair_sum(p, depth[rows, :])
            tc, t, j = fill(slot, t, j)
            upcoming.append(tc)
        return at_start, t, j, tuple(upcoming)

    first = jnp.where(count(first_tile) <= 2, 1, 0)
    t, j = first, 1
    at = []
    for slot in range(JOBS):
        tc, t, j = fill(slot, t, j)
        at.append(tc)
    lax.while_loop(lambda state: state[0] < tiles, jobs, (first, t, j, tuple(at)))
    for acc in accs:
        pltpu.matmul_pop(acc)


def own_kernel(counts_hbm, points_hbm, elements_hbm, pivots_hbm, message, out, lhs, tab, side, found,
               counts, points, elements, pivots, wide, depth, sems, *, accs):
    loads = [
        pltpu.make_async_copy(points_hbm, points, sems.at[0]),
        pltpu.make_async_copy(elements_hbm, elements, sems.at[1]),
        pltpu.make_async_copy(pivots_hbm, pivots, sems.at[2]),
        pltpu.make_async_copy(counts_hbm, counts, sems.at[3]),
    ]
    for load in loads:
        load.start()
    s = message[0:4]
    build_table(s, wide, tab)
    build_side(s, lax.axis_index("col") * TILE, side)
    for load in loads:
        load.wait()
    build_lhs(points, elements, lhs)
    find_pivots(points, pivots, message, found)
    pl.run_scoped(functools.partial(assemble, lambda t: counts[t], lhs, out, tab, side, depth, 0), *accs)


def rest_kernel(counts_hbm, lhs, message, own_tab, own_side, rest_out, root_out, tab, side,
                counts, scalars, wide, depth, sems, *, accs):
    loads = [
        pltpu.make_async_copy(counts_hbm, counts, sems.at[0]),
        pltpu.make_async_copy(message, scalars, sems.at[1]),
    ]
    for load in loads:
        load.start()
    s = message[0:4]
    build_table(s, wide, tab)
    build_side(s, 0, side)
    for load in loads:
        load.wait()
    early = (lhs.shape[0] - rest_out.shape[0]) // TILE

    def both(*accs):
        assemble(lambda t: counts[t], lhs, rest_out, own_tab, own_side, depth, early, *accs)
        assemble(lambda t: scalars[4, t].astype(I32), lhs, root_out, tab, side, depth, 0, *accs)

    pl.run_scoped(both, *accs)


def find_pivots(points, pivots, message, out):
    tiles = points.shape[1] // TILE
    piv = jnp.broadcast_to(pivots[...], (8, TILE))
    tile = jnp.right_shift(piv, 7) - lax.axis_index("row") * tiles
    lane = jnp.bitwise_and(piv, TILE - 1)
    inside = (tile >= 0) & (tile < tiles)
    found = jnp.zeros((8, TILE), F32)
    for t in range(tiles):
        pt = jnp.concatenate([points[:, t * TILE : (t + 1) * TILE], jnp.zeros((5, TILE), F32)], 0)
        got = jnp.take_along_axis(pt, lane, axis=1, mode="promise_in_bounds")
        found = jnp.where(tile == t, got, found)
    at = jnp.clip(tile, 0, tiles - 1)
    count = jnp.take_along_axis(message[...], at, axis=1, mode="promise_in_bounds")
    rows = lax.broadcasted_iota(I32, (8, TILE), 0)
    found = jnp.where((rows == 3) & inside, jnp.broadcast_to(count[4:5], (8, TILE)), found)
    out[...] = jnp.where((rows == 4) & inside, (tile + 1).astype(F32), found)


def pick_kernel(found, root, out):
    tile = jnp.broadcast_to(found[4:5], (8, TILE))
    at = jnp.maximum(tile.astype(I32) - 1, 0)
    count = jnp.take_along_axis(root[...], at, axis=1, mode="promise_in_bounds")
    rows = lax.broadcasted_iota(I32, (8, TILE), 0)
    count = jnp.where(tile > 0.0, jnp.broadcast_to(count[4:5], (8, TILE)), 0.0)
    out[...] = jnp.where(rows == 4, count, found[...])


def pivot_block(points, n_row, tab, side, right):
    f = point_features(points[0:1], points[1:2], points[2:3], [n_row])
    a = f.T.astype(BF)
    right[0:FEATS, 0:TILE] = side[:, 0:TILE]
    q = mm(a, right[...])
    dz = q[:, 0:TILE]
    dz2 = dz * dz
    n = q[:, TILE:]
    total = jnp.zeros((TILE, TILE), F32)
    for j in range(PAIRS):
        p = mm(a, tall(tab[j], TILE))
        for k in range(2):
            value = kernel_sum(p[:, k * TILE : (k + 1) * TILE], dz2)
            total = total + (value if 2 * j + k < 2 else jnp.where(n > 2 * j + k, value, 0.0))
    return total / n


def factor(x_ref, inv_ref, u_ref):
    side = TILE
    half = 8
    sub = lax.broadcasted_iota(I32, (half, TILE), 0)
    lane = lax.broadcasted_iota(I32, (half, TILE), 1)
    big = lax.broadcasted_iota(I32, (side, TILE), 0)
    inv_ref[...] = jnp.zeros_like(inv_ref)
    parts = range(BLOCK // half)

    def whole(rows):
        return jnp.broadcast_to(rows, (half, TILE))

    for b in range(side // BLOCK):
        k0 = b * BLOCK
        block = x_ref[:, k0 : k0 + BLOCK]
        high = block.astype(BF).astype(F32)
        a = jnp.concatenate([high, block - high, high], 1).astype(BF)
        left = [x_ref[k0 + half * i : k0 + half * (i + 1), 0:TILE] for i in parts]
        right = [x_ref[k0 + half * i : k0 + half * (i + 1), TILE:] for i in parts]
        cols = [[whole(v[:, k0 + j : k0 + j + 1]) for v in left] for j in range(BLOCK)]
        upper = [jnp.zeros((half, TILE), F32) for _ in parts]
        for j in range(BLOCK):
            f = cols[j]
            own, row = j // half, j % half
            here = sub == row
            inv = 1.0 / whole(f[own][row : row + 1, :])
            u_ref[k0 + j : k0 + j + 1, :] = right[own][row : row + 1, :]
            for i in parts:
                if i > own:
                    continue
                v = -f[i] * inv
                if i == own:
                    v = jnp.where(here, inv, jnp.where(sub < row, v, 0.0))
                upper[i] = jnp.where(lane == k0 + j, v, upper[i])

            def eliminate(v):
                pivot_row = whole(v[own][row : row + 1, :]) * inv
                rest = [v[i] - f[i] * pivot_row for i in parts]
                rest[own] = jnp.where(here, pivot_row, rest[own])
                return rest

            for jj in range(j + 1, BLOCK):
                cols[jj] = eliminate(cols[jj])
            left = eliminate(left)
            right = eliminate(right)

        def three(v):
            h, l = halves(v)
            return jnp.concatenate([h, h, l], 0)

        t = jnp.concatenate([jnp.concatenate(left, 0), jnp.concatenate(right, 0)], 1)
        prod = mm(a, three(t))
        for i in range(side // half):
            rows = slice(half * i, half * (i + 1))
            if k0 <= half * i < k0 + BLOCK:
                x_ref[rows, :] = t[half * i - k0 : half * (i + 1) - k0, :]
            else:
                x_ref[rows, :] = x_ref[rows, :] - prod[rows, :]
        v = jnp.concatenate(upper, 0)
        if k0:
            above = mm(a, three(v))
            inv_ref[0:k0, :] = inv_ref[0:k0, :] - above[0:k0, :]
        inv_ref[k0 : k0 + BLOCK, :] = v


def solve_kernel(picked, own_tab, own_side, root_tab, root_side, b_out, u_out, right, x, upper):
    is_root = lax.axis_index("col") == 0
    pk = picked[...]
    eye = (lax.broadcasted_iota(I32, (TILE, TILE), 0) == lax.broadcasted_iota(I32, (TILE, TILE), 1))
    right[:, 0:TILE] = jnp.zeros((TILE, TILE), BF)
    right[:, TILE:] = jnp.where(lax.broadcasted_iota(I32, (TILE, TILE), 0) == 24, 1.0, 0.0).astype(BF)
    x[:, 0:TILE] = pivot_block(pk, pk[4:5], root_tab, root_side, right) + jnp.where(eye, JUMP, 0.0)
    x[:, TILE:] = pivot_block(pk, pk[3:4], own_tab, own_side, right) + jnp.where(eye & is_root, JUMP, 0.0)
    factor(x, upper, u_out)
    wh, wl = halves(jnp.where(is_root, upper[...], -x[:, TILE:]))
    b_out[0:TILE, 0:TILE] = wh
    b_out[0:TILE, TILE:] = wl
    b_out[TILE:, 0:TILE] = wh
    b_out[TILE:, TILE:] = jnp.zeros_like(wl)


def apply_kernel(counts_hbm, message, b, own, rest, root, out_hbm, counts, scalars, ready, sems, out_sems, *, accs):
    tiles = root.shape[0] // TILE
    early = own.shape[0] // TILE
    loads = [
        pltpu.make_async_copy(counts_hbm, counts, sems.at[0]),
        pltpu.make_async_copy(message, scalars, sems.at[1]),
    ]
    for load in loads:
        load.start()
    keep = jnp.where(lax.axis_index("col") == 0, 0.0, 2.0)

    def out_copy(g):
        rows = pl.ds(pl.multiple_of(g * (WAYS * TILE), TILE), WAYS * TILE)
        return pltpu.make_async_copy(ready.at[rows, :], out_hbm.at[rows, :], out_sems.at[g])

    def product(*accs):
        for unit in range(2):
            pltpu.matmul_push_rhs(b[...], 0, unit)

        def begin(slot, t, first):
            h, l = halves(root[tile_rows(jnp.minimum(t, tiles - 1)), :])
            a = jnp.concatenate([h, l], 1)
            pltpu.matmul_acc_lhs(accs[slot], a, load_staged_rhs=0 if first else None)

        for slot in range(WAYS):
            begin(slot, slot, slot < 2)
        for load in loads:
            load.wait()

        def part(block, first):
            def group(g, carry):
                for slot in range(WAYS):
                    at = g * WAYS + slot
                    t = first + at
                    n0 = jnp.full((1, TILE), scalars[4, t], F32)
                    nc = jnp.full((1, TILE), counts[t], I32).astype(F32)
                    p = pltpu.matmul_pop(accs[slot])
                    prod = (p[:, 0:TILE] + p[:, TILE:]) * (2.0 / n0)
                    ready[tile_rows(t), :] = block[tile_rows(at), :] * (keep / nc) + prod
                    begin(slot, t + WAYS, False)
                out_copy(first // WAYS + g).start()
                return carry

            lax.fori_loop(0, block.shape[0] // TILE // WAYS, group, 0)

        part(own, 0)
        part(rest, early)
        for acc in accs:
            pltpu.matmul_pop(acc)

    pl.run_scoped(product, *accs[:WAYS])

    def finish(g, carry):
        out_copy(g).wait()
        return carry

    lax.fori_loop(0, tiles // WAYS, finish, 0)


def vmem():
    return pl.BlockSpec(memory_space=pltpu.VMEM)


def hbm():
    return pl.BlockSpec(memory_space=pltpu.HBM)


def numbered(send, steps):
    parts = []
    for k in steps:
        parts.append(send(k))
    return parts


def limit(mib):
    return pltpu.CompilerParams(vmem_limit_bytes=mib * 1024 * 1024)


def steps(accs, colloc_points, sources, counts, row_element, pivots):
    local_rows = colloc_points.shape[1]
    tiles = local_rows // TILE
    early = tiles // 2
    own_counts = counts.reshape(tiles)
    col = lax.axis_index("col")

    def stay(v):
        return pltpu.with_memory_space_constraint(v, pltpu.HBM)

    table = jax.ShapeDtypeStruct((2 * PAIRS + 1, FEATS, 2 * TILE), BF)
    aside = jax.ShapeDtypeStruct((FEATS, 2 * TILE), BF)

    def part(count):
        return jax.ShapeDtypeStruct((count * TILE, TILE), F32)

    wide = pltpu.VMEM((QUAD_MAX * FEATS, TILE), F32)
    message_block = jax.ShapeDtypeStruct((8, TILE), F32)
    scalar_counts = pltpu.SMEM((tiles,), I32)
    scalar_message = pltpu.SMEM((8, TILE), F32)

    message = pl.pallas_call(
        pack_kernel,
        out_shape=message_block,
        in_specs=[hbm()] * 2,
        out_specs=vmem(),
        scratch_shapes=[pltpu.VMEM((1, tiles), I32), pltpu.SemaphoreType.DMA((2,))],
        compiler_params=limit(4),
        name="pack",
    )(stay(sources), stay(own_counts.reshape(1, tiles)))
    got = numbered(lambda k: lax.ppermute(message, "col", [(0, k)]), (2, 1, 3))
    y_part = jnp.where(col == 0, message, got[0] + got[1] + got[2])
    got = numbered(lambda k: lax.ppermute(y_part, "col", [(i, i + k) for i in range(4)]), (8, 4, 12))
    root_message = jnp.where(col < 4, y_part, got[0] + got[1] + got[2])
    own_sum, lhs, own_tab, own_side, found = pl.pallas_call(
        functools.partial(own_kernel, accs=accs),
        out_shape=(part(early), jax.ShapeDtypeStruct((local_rows, TILE), BF), table, aside, message_block),
        in_specs=[hbm()] * 4 + [vmem()],
        out_specs=(vmem(),) * 5,
        scratch_shapes=[
            scalar_counts,
            pltpu.VMEM(colloc_points.shape, F32),
            pltpu.VMEM((tiles, TILE), I32),
            pltpu.VMEM((1, TILE), I32),
            wide,
            pltpu.VMEM((early * TILE, TILE), F32),
            pltpu.SemaphoreType.DMA((4,)),
        ],
        compiler_params=limit(12),
        name="own",
    )(
        stay(own_counts),
        stay(colloc_points),
        stay(row_element.reshape(tiles, TILE)),
        stay(pivots.reshape(1, TILE)),
        message,
    )
    picked = pl.pallas_call(
        pick_kernel,
        out_shape=message_block,
        in_specs=[vmem()] * 2,
        out_specs=vmem(),
        compiler_params=limit(4),
        name="pick",
    )(found, root_message)
    picked = picked + lax.ppermute(picked, "row", [(i, i ^ 1) for i in range(8)])
    got = numbered(lambda k: lax.ppermute(picked, "row", [(i, i ^ k) for i in range(8)]), (4, 2, 6))
    picked = picked + got[0] + got[1] + got[2]
    rest_sum, root_sum, root_tab, root_side = pl.pallas_call(
        functools.partial(rest_kernel, accs=accs),
        out_shape=(part(tiles - early), part(tiles), table, aside),
        in_specs=[hbm()] + [vmem()] * 4,
        out_specs=(vmem(),) * 4,
        scratch_shapes=[
            scalar_counts,
            scalar_message,
            wide,
            pltpu.VMEM((tiles * TILE, TILE), F32),
            pltpu.SemaphoreType.DMA((2,)),
        ],
        compiler_params=limit(20),
        name="rest",
    )(stay(own_counts), lhs, root_message, own_tab, own_side)
    factors, u_rows = pl.pallas_call(
        solve_kernel,
        out_shape=(
            jax.ShapeDtypeStruct((2 * TILE, 2 * TILE), BF),
            jax.ShapeDtypeStruct((TILE, TILE), F32),
        ),
        in_specs=[vmem()] * 5,
        out_specs=(vmem(), vmem()),
        scratch_shapes=[
            pltpu.VMEM((TILE, 2 * TILE), BF),
            pltpu.VMEM((TILE, 2 * TILE), F32),
            pltpu.VMEM((TILE, TILE), F32),
        ],
        compiler_params=limit(8),
        name="solve",
    )(picked, own_tab, own_side, root_tab, root_side)
    factored = pl.pallas_call(
        functools.partial(apply_kernel, accs=accs),
        out_shape=jax.ShapeDtypeStruct((local_rows, TILE), F32),
        in_specs=[hbm()] + [vmem()] * 5,
        out_specs=hbm(),
        scratch_shapes=[
            scalar_counts,
            scalar_message,
            pltpu.VMEM((local_rows, TILE), F32),
            pltpu.SemaphoreType.DMA((2,)),
            pltpu.SemaphoreType.DMA((tiles // WAYS,)),
        ],
        compiler_params=limit(20),
        name="apply",
    )(stay(own_counts), root_message, factors, own_sum, rest_sum, root_sum)
    return factored, u_rows


def body(accs, *args):
    return steps(accs, *args)


def solution(mesh):
    placed = (P(None, "row"), P(None, "col"), P("row", "col"), P("row"), P())
    with jax.sharding.use_abstract_mesh(mesh.abstract_mesh):
        accs = [pltpu.ACC(k % 2)((TILE, 2 * TILE), F32) for k in range(JOBS)]
    return jax.shard_map(
        functools.partial(body, accs),
        mesh=mesh,
        in_specs=placed,
        out_specs=(P("row", "col"), P(None, "col")),
        check_vma=False,
    )
```

time: 64.4 us -> 45.7 us (0.71)
  the two profiles are of different devices: /device:TPU:27 before, /device:TPU:1 now
where the time goes in v1:
time: 45.7 us; the launch traced here: 45.1 us
  Pallas kernels  24.7 us (54%)
  starting transfers between devices  18.1 us (40%)
  waiting for transfers between devices  1.55 us (3%)
  between operations  0.79 us (2%)
    pallas_call x1, Pallas kernels, steps(): pl.pallas_call(functools.partial(rest_kernel, accs=accs), out_shape=(part...  10.2 us
    ppermute x3, starting transfers between devices, steps(): got = numbered(lambda k: lax.ppermute(message, 'col', [(0, k)]), (2, 1, 3))  8.04 us
    pallas_call x1, Pallas kernels, steps(): pl.pallas_call(functools.partial(own_kernel, accs=accs), out_shape=(part(...  5.8 us
    pallas_call x1, Pallas kernels, steps(): pl.pallas_call(solve_kernel, out_shape=(jax.ShapeDtypeStruct((2 * TILE, 2...  4.96 us
    ppermute x3, starting transfers between devices, steps(): lax.ppermute(picked, 'row', [(i, i ^ k) for i in range(8)])  4.68 us
    ppermute x3, starting transfers between devices, steps(): lax.ppermute(y_part, 'col', [(i, i + k) for i in range(4)])  3.86 us
    pallas_call x1, Pallas kernels, steps(): pl.pallas_call(functools.partial(apply_kernel, accs=accs), out_shape=jax....  2.91 us
    ppermute x1, starting transfers between devices, steps(): lax.ppermute(picked, 'row', [(i, i ^ 1) for i in range(8)])  1.54 us
  transfers between devices with their start and end apart: 10, of which 2 were waited for; matrix products, arithmetic and copies ran while one was open for 0% of the time, Pallas kernels for 35%

profile of v1, /device:TPU:1, one launch (start us, length us, event | category | flops | bytes accessed | tf_op | source)
XLA Modules:
  0.0 45.1 jit_solution(13433983101997324294)
XLA Ops:
  0.6 0.7 %pack.1.message = f32[8,128]{1,0:T(8,128)S(1)} custom-call(f32[4,128]{1,0:T(4,128)} %sources_hbm.1, s32[1,60]{1,0:T(1,128)} %bitcast.5), custom_call_target="tpu_custom_call" | custom-call | tf_op jit(solution)/shard_map/pack/pallas_call | solution.py:521
  1.3 5.5 %collective-permute-start.2 = (f32[8,128]{1,0:T(8,128)S(1)}, f32[8,128]{1,0:T(8,128)S(1)}, u32[]{:S(2)}, u32[]{:S(2)}) collective-permute-start(f32[8,128]{1,0:T(8,128)S(1)} %pack.1.message), channel_id=1, source_target_pairs={{0,3},{16,19},{32,35},{48,51},{64,67},{80,83},{96,99},{112,115}} | collective-permute-start | bytes 12296 | tf_op jit(solution)/shard_map/ppermute | solution.py:530
  6.8 1.3 %collective-permute-start.1 = (f32[8,128]{1,0:T(8,128)S(1)}, f32[8,128]{1,0:T(8,128)S(1)}, u32[]{:S(2)}, u32[]{:S(2)}) collective-permute-start(f32[8,128]{1,0:T(8,128)S(1)} %pack.1.message), channel_id=1, source_target_pairs={{0,1},{16,17},{32,33},{48,49},{64,65},{80,81},{96,97},{112,113}} | collective-permute-start | bytes 12296 | tf_op jit(solution)/shard_map/ppermute | solution.py:530
  8.1 1.3 %collective-permute-start = (f32[8,128]{1,0:T(8,128)S(1)}, f32[8,128]{1,0:T(8,128)S(1)}, u32[]{:S(2)}, u32[]{:S(2)}) collective-permute-start(f32[8,128]{1,0:T(8,128)S(1)} %pack.1.message), channel_id=1, source_target_pairs={{0,2},{16,18},{32,34},{48,50},{64,66},{80,82},{96,98},{112,114}} | collective-permute-start | bytes 12296 | tf_op jit(solution)/shard_map/ppermute | solution.py:530
  9.4 0.0 collective-permute-done.2
  9.4 0.0 collective-permute-done.1
  9.4 0.7 %collective-permute-done = f32[8,128]{1,0:T(8,128)S(1)} collective-permute-done((f32[8,128]{1,0:T(8,128)S(1)}, f32[8,128]{1,0:T(8,128)S(1)}, u32[]{:S(2)}, u32[]{:S(2)}) %collective-permute-start) | collective-permute-done | bytes 4128 | tf_op jit(solution)/shard_map/ppermute | solution.py:530
  10.1 1.3 %collective-permute-start.5 = (f32[8,128]{1,0:T(8,128)S(1)}, f32[8,128]{1,0:T(8,128)S(1)}, u32[]{:S(2)}, u32[]{:S(2)}) collective-permute-start(f32[8,128]{1,0:T(8,128)S(1)} %add_select_fusion.1), channel_id=1, source_target_pairs={{0,12},{1,13},{2,14},{3,15},{16,28},{17,29},{18,30},{19,31},{32,44... | collective-permute-start | bytes 12296 | tf_op jit(solution)/shard_map/ppermute | solution.py:532
  11.4 1.3 %collective-permute-start.4 = (f32[8,128]{1,0:T(8,128)S(1)}, f32[8,128]{1,0:T(8,128)S(1)}, u32[]{:S(2)}, u32[]{:S(2)}) collective-permute-start(f32[8,128]{1,0:T(8,128)S(1)} %add_select_fusion.1), channel_id=1, source_target_pairs={{0,4},{1,5},{2,6},{3,7},{16,20},{17,21},{18,22},{19,23},{32,36},{3... | collective-permute-start | bytes 12296 | tf_op jit(solution)/shard_map/ppermute | solution.py:532
  12.7 1.3 %collective-permute-start.3 = (f32[8,128]{1,0:T(8,128)S(1)}, f32[8,128]{1,0:T(8,128)S(1)}, u32[]{:S(2)}, u32[]{:S(2)}) collective-permute-start(f32[8,128]{1,0:T(8,128)S(1)} %add_select_fusion.1), channel_id=1, source_target_pairs={{0,8},{1,9},{2,10},{3,11},{16,24},{17,25},{18,26},{19,27},{32,40},... | collective-permute-start | bytes 12296 | tf_op jit(solution)/shard_map/ppermute | solution.py:532
  14.0 5.8 %own.1 = (f32[3840,128]{1,0:T(8,128)S(1)}, bf16[7680,128]{1,0:T(8,128)(2,1)S(1)}, bf16[17,32,256]{2,1,0:T(8,128)(2,1)S(1)}, bf16[32,256]{1,0:T(8,128)(2,1)S(1)}, f32[8,128]{1,0:T(8,128)S(1)}) custom-call(s32[60]{0:T(128)} %bitcast.6, f32[3,7680]{1,0:T(4,128)} %points_hbm.1, s32[60,128]{1,0:T(8,128)} %bitcast.4, s32[1,128]{1,0:T(1,128)} %bitcast.9, ...), custom_call_target="tpu_custom_call" | custom-call | tf_op jit(solution)/shard_map/own/pallas_call | solution.py:534
  19.8 0.0 collective-permute-done.5
  19.9 0.0 collective-permute-done.4
  19.9 0.0 collective-permute-done.3
  19.9 0.1 pick.1
  20.0 1.5 %collective-permute-start.6 = (f32[8,128]{1,0:T(8,128)S(1)}, f32[8,128]{1,0:T(8,128)S(1)}, u32[]{:S(2)}, u32[]{:S(2)}) collective-permute-start(f32[8,128]{1,0:T(8,128)S(1)} %pick.1), channel_id=1, source_target_pairs={{0,16},{16,0},{32,48},{48,32},{64,80},{80,64},{96,112},{112,96},{1... | collective-permute-start | bytes 12296 | tf_op jit(solution)/shard_map/ppermute | solution.py:565
  21.5 0.8 %collective-permute-done.6 = f32[8,128]{1,0:T(8,128)S(1)} collective-permute-done((f32[8,128]{1,0:T(8,128)S(1)}, f32[8,128]{1,0:T(8,128)S(1)}, u32[]{:S(2)}, u32[]{:S(2)}) %collective-permute-start.6) | collective-permute-done | bytes 4128 | tf_op jit(solution)/shard_map/ppermute | solution.py:565
  22.3 3.5 %collective-permute-start.9 = (f32[8,128]{1,0:T(8,128)S(1)}, f32[8,128]{1,0:T(8,128)S(1)}, u32[]{:S(2)}, u32[]{:S(2)}) collective-permute-start(f32[8,128]{1,0:T(8,128)S(1)} %add.28), channel_id=1, source_target_pairs={{0,96},{16,112},{32,64},{48,80},{64,32},{80,48},{96,0},{112,16},{1... | collective-permute-start | bytes 12296 | tf_op jit(solution)/shard_map/ppermute | solution.py:566
  25.8 0.1 collective-permute-start.8
  25.9 1.1 %collective-permute-start.7 = (f32[8,128]{1,0:T(8,128)S(1)}, f32[8,128]{1,0:T(8,128)S(1)}, u32[]{:S(2)}, u32[]{:S(2)}) collective-permute-start(f32[8,128]{1,0:T(8,128)S(1)} %add.28), channel_id=1, source_target_pairs={{0,64},{16,80},{32,96},{48,112},{64,0},{80,16},{96,32},{112,48},{1... | collective-permute-start | bytes 12296 | tf_op jit(solution)/shard_map/ppermute | solution.py:566
  27.0 10.2 %rest.1 = (f32[3840,128]{1,0:T(8,128)S(1)}, f32[7680,128]{1,0:T(8,128)S(1)}, bf16[17,32,256]{2,1,0:T(8,128)(2,1)S(1)}, bf16[32,256]{1,0:T(8,128)(2,1)S(1)}) custom-call(s32[60]{0:T(128)} %bitcast.7, bf16[7680,128]{1,0:T(8,128)(2,1)S(1)} %get-tuple-element.16.lhs, f32[8,128]{1,0:T(8,128)S(1)} %add_select_fusion.root.message, ...), custom_call_target="tpu_custom_call" | custom-call | tf_op jit(solution)/shard_map/rest/pallas_call | solution.py:568
  37.2 0.0 collective-permute-done.9
  37.2 0.0 collective-permute-done.8
  37.2 0.0 collective-permute-done.7
  37.3 5.0 %solve.1 = (bf16[256,256]{1,0:T(8,128)(2,1)S(1)}, f32[128,128]{1,0:T(8,128)}) custom-call(f32[8,128]{1,0:T(8,128)S(1)} %add_add_fusion.picked, bf16[17,32,256]{2,1,0:T(8,128)(2,1)S(1)} %get-tuple-element.14.own_tab, bf16[32,256]{1,0:T(8,128)(2,1)S(1)} %get-tuple-element.15.own_side, bf16[17,32,256]{2,1,0:T(8,128)(2,1)S(1)} %get-tuple-element.17.root_tab, ...), custom_call_target="tpu_custom_call" | custom-call | tf_op jit(solution)/shard_map/solve/pallas_call | solution.py:583
  42.2 2.9 %apply.1 = f32[7680,128]{1,0:T(8,128)} custom-call(s32[60]{0:T(128)} %bitcast.8, f32[8,128]{1,0:T(8,128)S(1)} %add_select_fusion.root.message, bf16[256,256]{1,0:T(8,128)(2,1)S(1)} %get-tuple-element.19.b, f32[3840,128]{1,0:T(8,128)S(1)} %get-tuple-element.20.own, f32[3840,128]{1,0:T(8,128)S(1)} %get-tuple-element.21.rest, ...), custom_call_target="tpu_custom_call" | custom-call | tf_op jit(solution)/shard_map/apply/pallas_call | solution.py:599
  (4 shorter events, 0.0 us)
Async XLA Ops:
  1.3 8.1 %collective-permute-start.2 = (f32[8,128]{1,0:T(8,128)S(1)}, f32[8,128]{1,0:T(8,128)S(1)}, u32[]{:S(2)}, u32[]{:S(2)}) collective-permute-start(f32[8,128]{1,0:T(8,128)S(1)} %pack.1.message), channel_id=1, source_target_pairs={{0,3},{16,19},{32,35},{48,51},{64,67},{80,83},{96,99},{112,115}} | collective-permute-start | bytes 12296 | tf_op jit(solution)/shard_map/ppermute | solution.py:530
  6.8 2.6 %collective-permute-start.1 = (f32[8,128]{1,0:T(8,128)S(1)}, f32[8,128]{1,0:T(8,128)S(1)}, u32[]{:S(2)}, u32[]{:S(2)}) collective-permute-start(f32[8,128]{1,0:T(8,128)S(1)} %pack.1.message), channel_id=1, source_target_pairs={{0,1},{16,17},{32,33},{48,49},{64,65},{80,81},{96,97},{112,113}} | collective-permute-start | bytes 12296 | tf_op jit(solution)/shard_map/ppermute | solution.py:530
  8.1 2.0 %collective-permute-start = (f32[8,128]{1,0:T(8,128)S(1)}, f32[8,128]{1,0:T(8,128)S(1)}, u32[]{:S(2)}, u32[]{:S(2)}) collective-permute-start(f32[8,128]{1,0:T(8,128)S(1)} %pack.1.message), channel_id=1, source_target_pairs={{0,2},{16,18},{32,34},{48,50},{64,66},{80,82},{96,98},{112,114}} | collective-permute-start | bytes 12296 | tf_op jit(solution)/shard_map/ppermute | solution.py:530
  10.1 9.7 %collective-permute-start.5 = (f32[8,128]{1,0:T(8,128)S(1)}, f32[8,128]{1,0:T(8,128)S(1)}, u32[]{:S(2)}, u32[]{:S(2)}) collective-permute-start(f32[8,128]{1,0:T(8,128)S(1)} %add_select_fusion.1), channel_id=1, source_target_pairs={{0,12},{1,13},{2,14},{3,15},{16,28},{17,29},{18,30},{19,31},{32,44... | collective-permute-start | bytes 12296 | tf_op jit(solution)/shard_map/ppermute | solution.py:532
  11.4 8.4 %collective-permute-start.4 = (f32[8,128]{1,0:T(8,128)S(1)}, f32[8,128]{1,0:T(8,128)S(1)}, u32[]{:S(2)}, u32[]{:S(2)}) collective-permute-start(f32[8,128]{1,0:T(8,128)S(1)} %add_select_fusion.1), channel_id=1, source_target_pairs={{0,4},{1,5},{2,6},{3,7},{16,20},{17,21},{18,22},{19,23},{32,36},{3... | collective-permute-start | bytes 12296 | tf_op jit(solution)/shard_map/ppermute | solution.py:532
  12.7 7.1 %collective-permute-start.3 = (f32[8,128]{1,0:T(8,128)S(1)}, f32[8,128]{1,0:T(8,128)S(1)}, u32[]{:S(2)}, u32[]{:S(2)}) collective-permute-start(f32[8,128]{1,0:T(8,128)S(1)} %add_select_fusion.1), channel_id=1, source_target_pairs={{0,8},{1,9},{2,10},{3,11},{16,24},{17,25},{18,26},{19,27},{32,40},... | collective-permute-start | bytes 12296 | tf_op jit(solution)/shard_map/ppermute | solution.py:532
  20.0 2.4 %collective-permute-start.6 = (f32[8,128]{1,0:T(8,128)S(1)}, f32[8,128]{1,0:T(8,128)S(1)}, u32[]{:S(2)}, u32[]{:S(2)}) collective-permute-start(f32[8,128]{1,0:T(8,128)S(1)} %pick.1), channel_id=1, source_target_pairs={{0,16},{16,0},{32,48},{48,32},{64,80},{80,64},{96,112},{112,96},{1... | collective-permute-start | bytes 12296 | tf_op jit(solution)/shard_map/ppermute | solution.py:565
  22.3 14.9 %collective-permute-start.9 = (f32[8,128]{1,0:T(8,128)S(1)}, f32[8,128]{1,0:T(8,128)S(1)}, u32[]{:S(2)}, u32[]{:S(2)}) collective-permute-start(f32[8,128]{1,0:T(8,128)S(1)} %add.28), channel_id=1, source_target_pairs={{0,96},{16,112},{32,64},{48,80},{64,32},{80,48},{96,0},{112,16},{1... | collective-permute-start | bytes 12296 | tf_op jit(solution)/shard_map/ppermute | solution.py:566
  25.8 11.4 %collective-permute-start.8 = (f32[8,128]{1,0:T(8,128)S(1)}, f32[8,128]{1,0:T(8,128)S(1)}, u32[]{:S(2)}, u32[]{:S(2)}) collective-permute-start(f32[8,128]{1,0:T(8,128)S(1)} %add.28), channel_id=1, source_target_pairs={{0,32},{16,48},{32,0},{48,16},{64,96},{80,112},{96,64},{112,80},{1... | collective-permute-start | bytes 12296 | tf_op jit(solution)/shard_map/ppermute | solution.py:566
  25.9 11.4 %collective-permute-start.7 = (f32[8,128]{1,0:T(8,128)S(1)}, f32[8,128]{1,0:T(8,128)S(1)}, u32[]{:S(2)}, u32[]{:S(2)}) collective-permute-start(f32[8,128]{1,0:T(8,128)S(1)} %add.28), channel_id=1, source_target_pairs={{0,64},{16,80},{32,96},{48,112},{64,0},{80,16},{96,32},{112,48},{1... | collective-permute-start | bytes 12296 | tf_op jit(solution)/shard_map/ppermute | solution.py:566

commit v2 on v1

--- a/solution.py
+++ b/solution.py
@@ -23,6 +23,8 @@
 JOBS = 8
 DEPTH = 256
 WAYS = 6
+START = 3
+FAR = 1e30
 
 
 def split3(v):
@@ -92,19 +94,9 @@
         put(18 + k, one)
     for k, v in enumerate(split3(norm)):
         put(21 + k, v)
-    rows = lax.broadcasted_iota(I32, (FEATS, TILE), 0)
-    far = jnp.where(rows == 21, 1e30, 0.0).astype(BF)
     for q in range(QUAD_MAX):
-        block = wide_ref[pl.ds(FEATS * q, FEATS), :].astype(BF)
-        j = q // 2
-        if q % 2 == 0:
-            tab_ref[j, 0:FEATS, 0:TILE] = block
-            tab_ref[PAIRS + j, 0:FEATS, 0:TILE] = block
-            tab_ref[PAIRS + j, 0:FEATS, TILE:] = far
-        else:
-            tab_ref[j, 0:FEATS, TILE:] = block
-    tab_ref[2 * PAIRS, 0:FEATS, 0:TILE] = far
-    tab_ref[2 * PAIRS, 0:FEATS, TILE:] = far
+        columns = pl.ds(q % 2 * TILE, TILE)
+        tab_ref[q // 2, :, columns] = wide_ref[pl.ds(FEATS * q, FEATS), :].astype(BF)
 
 
 def depth_rows(s):
@@ -133,12 +125,6 @@
     return pl.ds(pl.multiple_of(t * TILE, TILE), TILE)
 
 
-def kernel_sum(p, dz2):
-    r = lax.rsqrt(p)
-    value = r * (2.0 + dz2 * (r * r))
-    return value
-
-
 def pair_sum(p, half):
     r = lax.rsqrt(p)
     cube = r * (r * r)
@@ -162,10 +148,13 @@
     lax.fori_loop(0, tiles // GROUP, group, 0)
 
 
-def pack_kernel(sources_hbm, counts_hbm, out, counts, sems):
+def pack_kernel(sources_hbm, counts_hbm, points_hbm, elements_hbm, pivots_hbm, out, points, elements, pivots, counts, sems):
     loads = [
         pltpu.make_async_copy(sources_hbm, out.at[pl.ds(0, 4), :], sems.at[0]),
         pltpu.make_async_copy(counts_hbm, counts, sems.at[1]),
+        pltpu.make_async_copy(points_hbm, points, sems.at[2]),
+        pltpu.make_async_copy(elements_hbm, elements, sems.at[3]),
+        pltpu.make_async_copy(pivots_hbm, pivots, sems.at[4]),
     ]
     for load in loads:
         load.start()
@@ -175,111 +164,126 @@
     out[4:5, 0 : counts.shape[1]] = counts[...].astype(F32)
 
 
-def wide_lhs(a):
-    return jnp.concatenate([a, jnp.zeros((a.shape[0], DEPTH - a.shape[1]), BF)], 1)
-
-
 def tall(b, rows):
     return jnp.concatenate([b, jnp.zeros((rows - b.shape[0], b.shape[1]), BF)], 0)
 
 
-def send(acc, a, b, slot):
-    pltpu.matmul_push_rhs(tall(b, DEPTH), slot // 2 % 2, slot % 2)
-    pltpu.matmul_acc_lhs(acc, wide_lhs(a), load_staged_rhs=slot // 2 % 2)
-
-
-def assemble(count, lhs, out, tab, side, depth, first_tile, *accs):
+def build_far(far_ref):
+    lane = lax.broadcasted_iota(I32, (TILE, TILE), 1)
+    far_ref[0] = jnp.zeros((TILE, TILE), BF)
+    far_ref[1] = jnp.where(lane == 0, FAR, 0.0).astype(BF)
+    far_ref[2] = jnp.where(lane < 2, FAR, 0.0).astype(BF)
+
+
+def pair_rhs(block):
+    rows = lax.broadcasted_iota(I32, (16, 2 * TILE), 0)
+    lane = lax.broadcasted_iota(I32, (16, 2 * TILE), 1)
+    pick = jnp.where(rows == 1 - lane // TILE, 1.0, 0.0).astype(BF)
+    return jnp.concatenate([tall(block, TILE), tall(pick, DEPTH - TILE)], 0)
+
+
+def assemble(count, lhs, out, weights, tab, side, depth, far, turns, sizes, first_tile, *accs):
     tiles = out.shape[0] // TILE
-
-    def begin(slot, t):
+    none = jnp.zeros((TILE, DEPTH - TILE), BF)
+
+    pltpu.matmul_push_rhs(tall(tab[0], DEPTH), 0, 0)
+    pltpu.matmul_push_rhs(tall(side[...], DEPTH), 0, 1)
+
+    def begin(slot, t, first):
         a = lhs[tile_rows(first_tile + jnp.minimum(t, tiles - 1)), :]
-        send(accs[2 * slot], a, tab[0], 2 * slot)
-        send(accs[2 * slot + 1], a, side[...], 2 * slot + 1)
-
-    def finish(slot, t):
-        p = pltpu.matmul_pop(accs[2 * slot])
-        q = pltpu.matmul_pop(accs[2 * slot + 1])
-        n = jnp.full((1, TILE), count(first_tile + t), I32).astype(F32)
-        half = q[:, 0:TILE] * (q[:, 0:TILE] * 0.5)
-        out[tile_rows(t), :] = pair_sum(p, half) + jnp.where(q[:, TILE:] == 0.0, (0.5 * JUMP) * n, 0.0)
-        depth[tile_rows(t), :] = half
-
-    ways = JOBS // 2
+        a = jnp.concatenate([a, none], 1)
+        pltpu.matmul_acc_lhs(accs[2 * slot], a, load_staged_rhs=0 if first else None)
+        pltpu.matmul_acc_lhs(accs[2 * slot + 1], a, load_staged_rhs=0 if first else None)
+
+    ways = START
     for slot in range(ways):
-        begin(slot, slot)
-
-    def start(g, carry):
+        begin(slot, slot, slot == 0)
+
+    def start(g, places, last=False):
         for slot in range(ways):
             t = g * ways + slot
-            finish(slot, jnp.minimum(t, tiles - 1))
-            begin(slot, t + ways)
-        return carry
-
-    lax.fori_loop(0, (tiles + ways - 1) // ways, start, 0)
-    for acc in accs:
-        pltpu.matmul_pop(acc)
-
-    def fill(slot, t, j):
-        tc = jnp.minimum(t, tiles - 1)
-        n = count(first_tile + tc)
-        index = jnp.where(2 * j + 1 < n, j, PAIRS + j)
-        index = jnp.where((t < tiles) & (2 * j < n), index, 2 * PAIRS)
-        send(accs[slot], lhs[tile_rows(first_tile + tc), :], tab[index], slot)
-        more = 2 * (j + 1) < n
-        short = count(first_tile + jnp.minimum(t + 1, tiles - 1)) <= 2
-        return tc, jnp.where(more, t, jnp.where(short, t + 2, t + 1)), jnp.where(more, j + 1, 1)
+            p = pltpu.matmul_pop(accs[2 * slot])
+            q = pltpu.matmul_pop(accs[2 * slot + 1])
+            points = count(first_tile + t)
+            n = jnp.full((1, TILE), points, I32).astype(F32)
+            weights[pl.ds(t, 1), :] = 2.0 / n
+            half = q[:, 0:TILE] * (q[:, 0:TILE] * 0.5)
+            out[tile_rows(t), :] = pair_sum(p, half) + jnp.where(q[:, TILE:] == 0.0, (0.5 * JUMP) * n, 0.0)
+            depth[tile_rows(t), :] = half
+            if not last:
+                begin(slot, t + ways, False)
+            after = []
+            for j in range(1, PAIRS):
+                turns[j, places[j - 1]] = t
+                after.append(places[j - 1] + jnp.where(points > 2 * j, 1, 0))
+            places = tuple(after)
+        return places
+
+    groups = tiles // ways
+    places = start(groups - 1, lax.fori_loop(0, groups - 1, start, (0,) * (PAIRS - 1)), True)
+    for j in range(1, PAIRS):
+        sizes[j] = places[j - 1]
+    sizes[PAIRS] = 0
+
+    def fill(j, g):
+        size = sizes[j]
+        b = pair_rhs(tab[jnp.minimum(j, PAIRS - 1)])
+        for unit in range(2):
+            pltpu.matmul_push_rhs(b, 0, unit)
+        at = []
+        for slot in range(JOBS):
+            place = g * JOBS + slot
+            t = turns[jnp.minimum(j, PAIRS - 1), jnp.maximum(jnp.minimum(place, size - 1), 0)]
+            t = jnp.clip(t, 0, tiles - 1)
+            points = count(first_tile + t)
+            index = jnp.where(place < size, jnp.where(points > 2 * j + 1, 0, 1), 2)
+            a = jnp.concatenate([lhs[tile_rows(first_tile + t), :], far[index]], 1)
+            pltpu.matmul_acc_lhs(accs[slot], a, load_staged_rhs=0 if slot < 2 else None)
+            at.append(t)
+        more = (g + 1) * JOBS < size
+        return jnp.where(more, j, jnp.minimum(j + 1, PAIRS)), jnp.where(more, g + 1, 0), tuple(at)
 
     def jobs(state):
-        _, t, j, at = state
-        upcoming = []
-        at_start = t
+        _, j, g, at = state
+        busy = sizes[j]
         for slot in range(JOBS):
             rows = tile_rows(at[slot])
             p = pltpu.matmul_pop(accs[slot])
             out[rows, :] = out[rows, :] + pair_sum(p, depth[rows, :])
-            tc, t, j = fill(slot, t, j)
-            upcoming.append(tc)
-        return at_start, t, j, tuple(upcoming)
-
-    first = jnp.where(count(first_tile) <= 2, 1, 0)
-    t, j = first, 1
-    at = []
-    for slot in range(JOBS):
-        tc, t, j = fill(slot, t, j)
-        at.append(tc)
-    lax.while_loop(lambda state: state[0] < tiles, jobs, (first, t, j, tuple(at)))
+        return (busy,) + fill(j, g)
+
+    lax.while_loop(lambda state: state[0] > 0, jobs, (sizes[1],) + fill(1, 0))
     for acc in accs:
         pltpu.matmul_pop(acc)
 
 
-def own_kernel(counts_hbm, points_hbm, elements_hbm, pivots_hbm, message, out, lhs, tab, side, found,
-               counts, points, elements, pivots, wide, depth, sems, *, accs):
-    loads = [
-        pltpu.make_async_copy(points_hbm, points, sems.at[0]),
-        pltpu.make_async_copy(elements_hbm, elements, sems.at[1]),
-        pltpu.make_async_copy(pivots_hbm, pivots, sems.at[2]),
-        pltpu.make_async_copy(counts_hbm, counts, sems.at[3]),
-    ]
-    for load in loads:
-        load.start()
+def own_kernel(counts_hbm, points, elements, pivots, message, out, weights, lhs, tab, side, found,
+               counts, wide, depth, far, turns, sizes, sem, *, accs):
+    load = pltpu.make_async_copy(counts_hbm, counts, sem)
+    load.start()
     s = message[0:4]
     build_table(s, wide, tab)
     build_side(s, lax.axis_index("col") * TILE, side)
-    for load in loads:
-        load.wait()
+    build_far(far)
     build_lhs(points, elements, lhs)
     find_pivots(points, pivots, message, found)
-    pl.run_scoped(functools.partial(assemble, lambda t: counts[t], lhs, out, tab, side, depth, 0), *accs)
-
-
-def rest_kernel(counts_hbm, lhs, message, own_tab, own_side, rest_out, root_out, tab, side,
-                counts, scalars, wide, depth, sems, *, accs):
+    load.wait()
+    lists = (depth, far, turns, sizes)
+
+    @pl.when(lax.axis_index("col") != 0)
+    def _():
+        pl.run_scoped(functools.partial(assemble, lambda t: counts[t], lhs, out, weights, tab, side, *lists, 0), *accs)
+
+
+def rest_kernel(counts_hbm, lhs, message, own_tab, own_side, rest_out, rest_weights, root_out, root_weights, tab, side,
+                counts, scalars, wide, depth, far, turns, sizes, sems, *, accs):
     loads = [
         pltpu.make_async_copy(counts_hbm, counts, sems.at[0]),
         pltpu.make_async_copy(message, scalars, sems.at[1]),
     ]
     for load in loads:
         load.start()
+    build_far(far)
     s = message[0:4]
     build_table(s, wide, tab)
     build_side(s, 0, side)
@@ -288,8 +292,13 @@
     early = (lhs.shape[0] - rest_out.shape[0]) // TILE
 
     def both(*accs):
-        assemble(lambda t: counts[t], lhs, rest_out, own_tab, own_side, depth, early, *accs)
-        assemble(lambda t: scalars[4, t].astype(I32), lhs, root_out, tab, side, depth, 0, *accs)
+        lists = (depth, far, turns, sizes)
+
+        @pl.when(lax.axis_index("col") != 0)
+        def _():
+            assemble(lambda t: counts[t], lhs, rest_out, rest_weights, own_tab, own_side, *lists, early, *accs)
+
+        assemble(lambda t: scalars[4, t].astype(I32), lhs, root_out, root_weights, tab, side, *lists, 0, *accs)
 
     pl.run_scoped(both, *accs)
 
@@ -323,19 +332,19 @@
 
 def pivot_block(points, n_row, tab, side, right):
     f = point_features(points[0:1], points[1:2], points[2:3], [n_row])
+    numbers = lax.broadcasted_iota(I32, (QUAD_MAX, TILE), 0)
+    absent = jnp.where(numbers.astype(F32) >= n_row, FAR, 0.0)
+    f = jnp.concatenate([f[0:FEATS], absent, f[FEATS + QUAD_MAX :]], 0)
     a = f.T.astype(BF)
     right[0:FEATS, 0:TILE] = side[:, 0:TILE]
     q = mm(a, right[...])
-    dz = q[:, 0:TILE]
-    dz2 = dz * dz
-    n = q[:, TILE:]
+    half = q[:, 0:TILE] * (q[:, 0:TILE] * 0.5)
+    numbers = lax.broadcasted_iota(I32, (QUAD_MAX, 2 * TILE), 0) - lax.broadcasted_iota(I32, (QUAD_MAX, 2 * TILE), 1) // TILE
     total = jnp.zeros((TILE, TILE), F32)
     for j in range(PAIRS):
-        p = mm(a, tall(tab[j], TILE))
-        for k in range(2):
-            value = kernel_sum(p[:, k * TILE : (k + 1) * TILE], dz2)
-            total = total + (value if 2 * j + k < 2 else jnp.where(n > 2 * j + k, value, 0.0))
-    return total / n
+        pick = jnp.where(numbers == 2 * j, 1.0, 0.0).astype(BF)
+        total = total + pair_sum(mm(a, tall(jnp.concatenate([tab[j], pick], 0), TILE)), half)
+    return total * (2.0 / q[:, TILE:])
 
 
 def factor(x_ref, inv_ref, u_ref):
@@ -419,16 +428,10 @@
     b_out[TILE:, TILE:] = jnp.zeros_like(wl)
 
 
-def apply_kernel(counts_hbm, message, b, own, rest, root, out_hbm, counts, scalars, ready, sems, out_sems, *, accs):
+def apply_kernel(b, own, own_weights, rest, rest_weights, root, root_weights, out_hbm, ready, out_sems, *, accs):
     tiles = root.shape[0] // TILE
     early = own.shape[0] // TILE
-    loads = [
-        pltpu.make_async_copy(counts_hbm, counts, sems.at[0]),
-        pltpu.make_async_copy(message, scalars, sems.at[1]),
-    ]
-    for load in loads:
-        load.start()
-    keep = jnp.where(lax.axis_index("col") == 0, 0.0, 2.0)
+    is_root = lax.axis_index("col") == 0
 
     def out_copy(g):
         rows = pl.ds(pl.multiple_of(g * (WAYS * TILE), TILE), WAYS * TILE)
@@ -445,27 +448,24 @@
 
         for slot in range(WAYS):
             begin(slot, slot, slot < 2)
-        for load in loads:
-            load.wait()
-
-        def part(block, first):
+
+        def part(block, weights, first):
             def group(g, carry):
                 for slot in range(WAYS):
                     at = g * WAYS + slot
                     t = first + at
-                    n0 = jnp.full((1, TILE), scalars[4, t], F32)
-                    nc = jnp.full((1, TILE), counts[t], I32).astype(F32)
                     p = pltpu.matmul_pop(accs[slot])
-                    prod = (p[:, 0:TILE] + p[:, TILE:]) * (2.0 / n0)
-                    ready[tile_rows(t), :] = block[tile_rows(at), :] * (keep / nc) + prod
+                    prod = (p[:, 0:TILE] + p[:, TILE:]) * root_weights[pl.ds(t, 1), :]
+                    base = jnp.where(is_root, 0.0, block[tile_rows(at), :] * weights[pl.ds(at, 1), :])
+                    ready[tile_rows(t), :] = base + prod
                     begin(slot, t + WAYS, False)
                 out_copy(first // WAYS + g).start()
                 return carry
 
             lax.fori_loop(0, block.shape[0] // TILE // WAYS, group, 0)
 
-        part(own, 0)
-        part(rest, early)
+        part(own, own_weights, 0)
+        part(rest, rest_weights, early)
         for acc in accs:
             pltpu.matmul_pop(acc)
 
@@ -507,53 +507,54 @@
     def stay(v):
         return pltpu.with_memory_space_constraint(v, pltpu.HBM)
 
-    table = jax.ShapeDtypeStruct((2 * PAIRS + 1, FEATS, 2 * TILE), BF)
+    table = jax.ShapeDtypeStruct((PAIRS, FEATS, 2 * TILE), BF)
     aside = jax.ShapeDtypeStruct((FEATS, 2 * TILE), BF)
 
     def part(count):
         return jax.ShapeDtypeStruct((count * TILE, TILE), F32)
+
+    def rows(count):
+        return jax.ShapeDtypeStruct((count, TILE), F32)
 
     wide = pltpu.VMEM((QUAD_MAX * FEATS, TILE), F32)
     message_block = jax.ShapeDtypeStruct((8, TILE), F32)
     scalar_counts = pltpu.SMEM((tiles,), I32)
     scalar_message = pltpu.SMEM((8, TILE), F32)
-
-    message = pl.pallas_call(
+    lists = [pltpu.VMEM((3, TILE, TILE), BF), pltpu.SMEM((PAIRS, tiles + 1), I32), pltpu.SMEM((PAIRS + 1,), I32)]
+
+    message, points, elements, pivot_row = pl.pallas_call(
         pack_kernel,
-        out_shape=message_block,
-        in_specs=[hbm()] * 2,
-        out_specs=vmem(),
-        scratch_shapes=[pltpu.VMEM((1, tiles), I32), pltpu.SemaphoreType.DMA((2,))],
+        out_shape=(
+            message_block,
+            jax.ShapeDtypeStruct(colloc_points.shape, F32),
+            jax.ShapeDtypeStruct((tiles, TILE), I32),
+            jax.ShapeDtypeStruct((1, TILE), I32),
+        ),
+        in_specs=[hbm()] * 5,
+        out_specs=(vmem(),) * 4,
+        scratch_shapes=[pltpu.VMEM((1, tiles), I32), pltpu.SemaphoreType.DMA((5,))],
         compiler_params=limit(4),
         name="pack",
-    )(stay(sources), stay(own_counts.reshape(1, tiles)))
-    got = numbered(lambda k: lax.ppermute(message, "col", [(0, k)]), (2, 1, 3))
-    y_part = jnp.where(col == 0, message, got[0] + got[1] + got[2])
-    got = numbered(lambda k: lax.ppermute(y_part, "col", [(i, i + k) for i in range(4)]), (8, 4, 12))
-    root_message = jnp.where(col < 4, y_part, got[0] + got[1] + got[2])
-    own_sum, lhs, own_tab, own_side, found = pl.pallas_call(
-        functools.partial(own_kernel, accs=accs),
-        out_shape=(part(early), jax.ShapeDtypeStruct((local_rows, TILE), BF), table, aside, message_block),
-        in_specs=[hbm()] * 4 + [vmem()],
-        out_specs=(vmem(),) * 5,
-        scratch_shapes=[
-            scalar_counts,
-            pltpu.VMEM(colloc_points.shape, F32),
-            pltpu.VMEM((tiles, TILE), I32),
-            pltpu.VMEM((1, TILE), I32),
-            wide,
-            pltpu.VMEM((early * TILE, TILE), F32),
-            pltpu.SemaphoreType.DMA((4,)),
-        ],
-        compiler_params=limit(12),
-        name="own",
     )(
-        stay(own_counts),
+        stay(sources),
+        stay(own_counts.reshape(1, tiles)),
         stay(colloc_points),
         stay(row_element.reshape(tiles, TILE)),
         stay(pivots.reshape(1, TILE)),
-        message,
     )
+    got = numbered(lambda k: lax.ppermute(message, "col", [(0, k)]), (2, 3, 1))
+    y_part = jnp.where(col == 0, message, got[0] + got[1] + got[2])
+    got = numbered(lambda k: lax.ppermute(y_part, "col", [(i, i + k) for i in range(4)]), (8, 12, 4))
+    root_message = jnp.where(col < 4, y_part, got[0] + got[1] + got[2])
+    own_sum, own_weights, lhs, own_tab, own_side, found = pl.pallas_call(
+        functools.partial(own_kernel, accs=accs),
+        out_shape=(part(early), rows(early), jax.ShapeDtypeStruct((local_rows, TILE), BF), table, aside, message_block),
+        in_specs=[hbm()] + [vmem()] * 4,
+        out_specs=(vmem(),) * 6,
+        scratch_shapes=[scalar_counts, wide, pltpu.VMEM((early * TILE, TILE), F32), *lists, pltpu.SemaphoreType.DMA],
+        compiler_params=limit(12),
+        name="own",
+    )(stay(own_counts), points, elements, pivot_row, message)
     picked = pl.pallas_call(
         pick_kernel,
         out_shape=message_block,
@@ -565,16 +566,17 @@
     picked = picked + lax.ppermute(picked, "row", [(i, i ^ 1) for i in range(8)])
     got = numbered(lambda k: lax.ppermute(picked, "row", [(i, i ^ k) for i in range(8)]), (4, 2, 6))
     picked = picked + got[0] + got[1] + got[2]
-    rest_sum, root_sum, root_tab, root_side = pl.pallas_call(
+    rest_sum, rest_weights, root_sum, root_weights, root_tab, root_side = pl.pallas_call(
         functools.partial(rest_kernel, accs=accs),
-        out_shape=(part(tiles - early), part(tiles), table, aside),
+        out_shape=(part(tiles - early), rows(tiles - early), part(tiles), rows(tiles), table, aside),
         in_specs=[hbm()] + [vmem()] * 4,
-        out_specs=(vmem(),) * 4,
+        out_specs=(vmem(),) * 6,
         scratch_shapes=[
             scalar_counts,
             scalar_message,
             wide,
             pltpu.VMEM((tiles * TILE, TILE), F32),
+            *lists,
             pltpu.SemaphoreType.DMA((2,)),
         ],
         compiler_params=limit(20),
@@ -599,18 +601,12 @@
     factored = pl.pallas_call(
         functools.partial(apply_kernel, accs=accs),
         out_shape=jax.ShapeDtypeStruct((local_rows, TILE), F32),
-        in_specs=[hbm()] + [vmem()] * 5,
+        in_specs=[vmem()] * 7,
         out_specs=hbm(),
-        scratch_shapes=[
-            scalar_counts,
-            scalar_message,
-            pltpu.VMEM((local_rows, TILE), F32),
-            pltpu.SemaphoreType.DMA((2,)),
-            pltpu.SemaphoreType.DMA((tiles // WAYS,)),
-        ],
+        scratch_shapes=[pltpu.VMEM((local_rows, TILE), F32), pltpu.SemaphoreType.DMA((tiles // WAYS,))],
         compiler_params=limit(20),
         name="apply",
-    )(stay(own_counts), root_message, factors, own_sum, rest_sum, root_sum)
+    )(factors, own_sum, own_weights, rest_sum, rest_weights, root_sum, root_weights)
     return factored, u_rows
 
 

time: 45.7 us -> 45.3 us (level)
  the two profiles are of different devices: /device:TPU:1 before, /device:TPU:27 now
where the time goes in v2:
time: 45.3 us; the launch traced here: 45.1 us
  Pallas kernels  34.6 us (76%)
  starting transfers between devices  8.48 us (19%)
  waiting for transfers between devices  1.18 us (3%)
  between operations  0.82 us (2%)
    pallas_call x1, Pallas kernels, steps(): pl.pallas_call(functools.partial(rest_kernel, accs=accs), out_shape=(part...  16.1 us
    pallas_call x1, Pallas kernels, steps(): pl.pallas_call(functools.partial(own_kernel, accs=accs), out_shape=(part(...  10.3 us
    pallas_call x1, Pallas kernels, steps(): pl.pallas_call(solve_kernel, out_shape=(jax.ShapeDtypeStruct((2 * TILE, 2...  4.72 us
    ppermute x3, starting transfers between devices, steps(): lax.ppermute(picked, 'row', [(i, i ^ k) for i in range(8)])  3.85 us
    ppermute x3, starting transfers between devices, steps(): lax.ppermute(y_part, 'col', [(i, i + k) for i in range(4)])  2.62 us
    pallas_call x1, Pallas kernels, steps(): pl.pallas_call(functools.partial(apply_kernel, accs=accs), out_shape=jax....  2.38 us
    ppermute x3, starting transfers between devices, steps(): got = numbered(lambda k: lax.ppermute(message, 'col', [(0, k)]), (2, 3, 1))  1.98 us
    ppermute x1, waiting for transfers between devices, steps(): lax.ppermute(picked, 'row', [(i, i ^ 1) for i in range(8)])  1.15 us
  transfers between devices with their start and end apart: 10, of which 1 were waited for; matrix products, arithmetic and copies ran while one was open for 0% of the time, Pallas kernels for 59%

profile of v2, /device:TPU:27, one launch (start us, length us, event | category | flops | bytes accessed | tf_op | source)
XLA Modules:
  0.0 45.1 jit_solution(17783033183344838818)
XLA Ops:
  0.6 1.0 %pack.1 = (f32[8,128]{1,0:T(8,128)S(1)}, f32[3,7680]{1,0:T(4,128)S(1)}, s32[60,128]{1,0:T(8,128)S(1)}, s32[1,128]{1,0:T(1,128)S(1)}) custom-call(f32[4,128]{1,0:T(4,128)} %sources_hbm.1, s32[1,60]{1,0:T(1,128)} %bitcast.5, f32[3,7680]{1,0:T(4,128)} %points_hbm.1, s32[60,128]{1,0:T(8,128)} %bitcast.4, s32[1,128]{1,0:T(1,128)} %bitcast.8), custom_call_target="tpu_custom_call" | custom-call | tf_op jit(solution)/shard_map/pack/pallas_call | solution.py:525
  1.6 0.7 %collective-permute-start.2 = (f32[8,128]{1,0:T(8,128)S(1)}, f32[8,128]{1,0:T(8,128)S(1)}, u32[]{:S(2)}, u32[]{:S(2)}) collective-permute-start(f32[8,128]{1,0:T(8,128)S(1)} %get-tuple-element.23.message), channel_id=1, source_target_pairs={{0,1},{16,17},{32,33},{48,49},{64,65},{80,81},{96,97},{112,113}} | collective-permute-start | bytes 12296 | tf_op jit(solution)/shard_map/ppermute | solution.py:545
  2.3 0.7 %collective-permute-start.1 = (f32[8,128]{1,0:T(8,128)S(1)}, f32[8,128]{1,0:T(8,128)S(1)}, u32[]{:S(2)}, u32[]{:S(2)}) collective-permute-start(f32[8,128]{1,0:T(8,128)S(1)} %get-tuple-element.23.message), channel_id=1, source_target_pairs={{0,3},{16,19},{32,35},{48,51},{64,67},{80,83},{96,99},{112,115}} | collective-permute-start | bytes 12296 | tf_op jit(solution)/shard_map/ppermute | solution.py:545
  3.0 0.7 %collective-permute-start = (f32[8,128]{1,0:T(8,128)S(1)}, f32[8,128]{1,0:T(8,128)S(1)}, u32[]{:S(2)}, u32[]{:S(2)}) collective-permute-start(f32[8,128]{1,0:T(8,128)S(1)} %get-tuple-element.23.message), channel_id=1, source_target_pairs={{0,2},{16,18},{32,34},{48,50},{64,66},{80,82},{96,98},{112,114}} | collective-permute-start | bytes 12296 | tf_op jit(solution)/shard_map/ppermute | solution.py:545
  3.6 0.0 collective-permute-done.2
  3.6 0.0 collective-permute-done.1
  3.7 0.0 collective-permute-done
  3.7 1.3 %collective-permute-start.5 = (f32[8,128]{1,0:T(8,128)S(1)}, f32[8,128]{1,0:T(8,128)S(1)}, u32[]{:S(2)}, u32[]{:S(2)}) collective-permute-start(f32[8,128]{1,0:T(8,128)S(1)} %add_select_fusion.1), channel_id=1, source_target_pairs={{0,4},{1,5},{2,6},{3,7},{16,20},{17,21},{18,22},{19,23},{32,36},{3... | collective-permute-start | bytes 12296 | tf_op jit(solution)/shard_map/ppermute | solution.py:547
  5.0 0.7 %collective-permute-start.4 = (f32[8,128]{1,0:T(8,128)S(1)}, f32[8,128]{1,0:T(8,128)S(1)}, u32[]{:S(2)}, u32[]{:S(2)}) collective-permute-start(f32[8,128]{1,0:T(8,128)S(1)} %add_select_fusion.1), channel_id=1, source_target_pairs={{0,12},{1,13},{2,14},{3,15},{16,28},{17,29},{18,30},{19,31},{32,44... | collective-permute-start | bytes 12296 | tf_op jit(solution)/shard_map/ppermute | solution.py:547
  5.7 0.7 %collective-permute-start.3 = (f32[8,128]{1,0:T(8,128)S(1)}, f32[8,128]{1,0:T(8,128)S(1)}, u32[]{:S(2)}, u32[]{:S(2)}) collective-permute-start(f32[8,128]{1,0:T(8,128)S(1)} %add_select_fusion.1), channel_id=1, source_target_pairs={{0,8},{1,9},{2,10},{3,11},{16,24},{17,25},{18,26},{19,27},{32,40},... | collective-permute-start | bytes 12296 | tf_op jit(solution)/shard_map/ppermute | solution.py:547
  6.3 10.3 %own.1 = (f32[3840,128]{1,0:T(8,128)S(1)}, f32[30,128]{1,0:T(8,128)S(1)}, bf16[7680,128]{1,0:T(8,128)(2,1)S(1)}, bf16[8,32,256]{2,1,0:T(8,128)(2,1)S(1)}, bf16[3...) custom-call(s32[60]{0:T(128)} %bitcast.6, f32[3,7680]{1,0:T(4,128)S(1)} %get-tuple-element.20.points, ...), custom_call_target="tpu_custom_call" | custom-call | tf_op jit(solution)/shard_map/own/pallas_call | solution.py:549
  16.7 0.0 collective-permute-done.5
  16.7 0.0 collective-permute-done.4
  16.7 0.0 collective-permute-done.3
  16.7 0.1 pick.1
  16.8 0.0 collective-permute-start.6
  16.8 1.2 %collective-permute-done.6 = f32[8,128]{1,0:T(8,128)S(1)} collective-permute-done((f32[8,128]{1,0:T(8,128)S(1)}, f32[8,128]{1,0:T(8,128)S(1)}, u32[]{:S(2)}, u32[]{:S(2)}) %collective-permute-start.6) | collective-permute-done | bytes 4128 | tf_op jit(solution)/shard_map/ppermute | solution.py:566
  18.0 0.0 collective-permute-start.9
  18.0 0.0 collective-permute-start.8
  18.0 3.8 %collective-permute-start.7 = (f32[8,128]{1,0:T(8,128)S(1)}, f32[8,128]{1,0:T(8,128)S(1)}, u32[]{:S(2)}, u32[]{:S(2)}) collective-permute-start(f32[8,128]{1,0:T(8,128)S(1)} %add.28), channel_id=1, source_target_pairs={{0,64},{16,80},{32,96},{48,112},{64,0},{80,16},{96,32},{112,48},{1... | collective-permute-start | bytes 12296 | tf_op jit(solution)/shard_map/ppermute | solution.py:567
  21.8 16.1 %rest.1 = (f32[3840,128]{1,0:T(8,128)S(1)}, f32[30,128]{1,0:T(8,128)S(1)}, f32[7680,128]{1,0:T(8,128)S(1)}, f32[60,128]{1,0:T(8,128)S(1)}, bf16[8,32,256]{2,1,0:T(8,128)(2,1)S(1)}, /*index=5*/bf16[32,256]{1,0:T(8,128)(2,1)S(1)}) custom-call(s32[60]{0:T(128)} %bitcast.7, bf16[7680,128]{1,0:T(8,128)(2,1)S(1)} %get-tuple-element.27.lhs, ...), custom_call_target="tpu_custom_call" | custom-call | tf_op jit(solution)/shard_map/rest/pallas_call | solution.py:569
  37.9 0.0 collective-permute-done.9
  37.9 0.0 collective-permute-done.8
  38.0 0.0 collective-permute-done.7
  38.0 4.7 %solve.1 = (bf16[256,256]{1,0:T(8,128)(2,1)S(1)}, f32[128,128]{1,0:T(8,128)}) custom-call(f32[8,128]{1,0:T(8,128)S(1)} %add_add_fusion.picked, bf16[8,32,256]{2,1,0:T(8,128)(2,1)S(1)} %get-tuple-element.25.own_tab, bf16[32,256]{1,0:T(8,128)(2,1)S(1)} %get-tuple-element.26.own_side, bf16[8,32,256]{2,1,0:T(8,128)(2,1)S(1)} %get-tuple-element.28.root_tab, ...), custom_call_target="tpu_custom_call" | custom-call | tf_op jit(solution)/shard_map/solve/pallas_call | solution.py:585
  42.7 2.4 %apply.1 = f32[7680,128]{1,0:T(8,128)} custom-call(bf16[256,256]{1,0:T(8,128)(2,1)S(1)} %get-tuple-element.30.b, f32[3840,128]{1,0:T(8,128)S(1)} %get-tuple-element.31.own, f32[30,128]{1,0:T(8,128)S(1)} %get-tuple-element.32.own_weights, f32[3840,128]{1,0:T(8,128)S(1)} %get-tuple-element.33.rest, f32[30,128]{1,0:T(8,128)S(1)} %get-tuple-element.34.rest_weights, ...), custom_call_target="tpu_custom_call" | custom-call | tf_op jit(solution)/shard_map/apply/pallas_call | solution.py:601
  (4 shorter events, 0.0 us)
Async XLA Ops:
  1.6 2.0 %collective-permute-start.2 = (f32[8,128]{1,0:T(8,128)S(1)}, f32[8,128]{1,0:T(8,128)S(1)}, u32[]{:S(2)}, u32[]{:S(2)}) collective-permute-start(f32[8,128]{1,0:T(8,128)S(1)} %get-tuple-element.23.message), channel_id=1, source_target_pairs={{0,1},{16,17},{32,33},{48,49},{64,65},{80,81},{96,97},{112,113}} | collective-permute-start | bytes 12296 | tf_op jit(solution)/shard_map/ppermute | solution.py:545
  2.3 1.4 %collective-permute-start.1 = (f32[8,128]{1,0:T(8,128)S(1)}, f32[8,128]{1,0:T(8,128)S(1)}, u32[]{:S(2)}, u32[]{:S(2)}) collective-permute-start(f32[8,128]{1,0:T(8,128)S(1)} %get-tuple-element.23.message), channel_id=1, source_target_pairs={{0,3},{16,19},{32,35},{48,51},{64,67},{80,83},{96,99},{112,115}} | collective-permute-start | bytes 12296 | tf_op jit(solution)/shard_map/ppermute | solution.py:545
  3.0 0.7 %collective-permute-start = (f32[8,128]{1,0:T(8,128)S(1)}, f32[8,128]{1,0:T(8,128)S(1)}, u32[]{:S(2)}, u32[]{:S(2)}) collective-permute-start(f32[8,128]{1,0:T(8,128)S(1)} %get-tuple-element.23.message), channel_id=1, source_target_pairs={{0,2},{16,18},{32,34},{48,50},{64,66},{80,82},{96,98},{112,114}} | collective-permute-start | bytes 12296 | tf_op jit(solution)/shard_map/ppermute | solution.py:545
  3.7 13.0 %collective-permute-start.5 = (f32[8,128]{1,0:T(8,128)S(1)}, f32[8,128]{1,0:T(8,128)S(1)}, u32[]{:S(2)}, u32[]{:S(2)}) collective-permute-start(f32[8,128]{1,0:T(8,128)S(1)} %add_select_fusion.1), channel_id=1, source_target_pairs={{0,4},{1,5},{2,6},{3,7},{16,20},{17,21},{18,22},{19,23},{32,36},{3... | collective-permute-start | bytes 12296 | tf_op jit(solution)/shard_map/ppermute | solution.py:547
  5.0 11.7 %collective-permute-start.4 = (f32[8,128]{1,0:T(8,128)S(1)}, f32[8,128]{1,0:T(8,128)S(1)}, u32[]{:S(2)}, u32[]{:S(2)}) collective-permute-start(f32[8,128]{1,0:T(8,128)S(1)} %add_select_fusion.1), channel_id=1, source_target_pairs={{0,12},{1,13},{2,14},{3,15},{16,28},{17,29},{18,30},{19,31},{32,44... | collective-permute-start | bytes 12296 | tf_op jit(solution)/shard_map/ppermute | solution.py:547
  5.7 11.0 %collective-permute-start.3 = (f32[8,128]{1,0:T(8,128)S(1)}, f32[8,128]{1,0:T(8,128)S(1)}, u32[]{:S(2)}, u32[]{:S(2)}) collective-permute-start(f32[8,128]{1,0:T(8,128)S(1)} %add_select_fusion.1), channel_id=1, source_target_pairs={{0,8},{1,9},{2,10},{3,11},{16,24},{17,25},{18,26},{19,27},{32,40},... | collective-permute-start | bytes 12296 | tf_op jit(solution)/shard_map/ppermute | solution.py:547
  16.8 1.2 %collective-permute-start.6 = (f32[8,128]{1,0:T(8,128)S(1)}, f32[8,128]{1,0:T(8,128)S(1)}, u32[]{:S(2)}, u32[]{:S(2)}) collective-permute-start(f32[8,128]{1,0:T(8,128)S(1)} %pick.1), channel_id=1, source_target_pairs={{0,16},{16,0},{32,48},{48,32},{64,80},{80,64},{96,112},{112,96},{1... | collective-permute-start | bytes 12296 | tf_op jit(solution)/shard_map/ppermute | solution.py:566
  18.0 20.0 %collective-permute-start.9 = (f32[8,128]{1,0:T(8,128)S(1)}, f32[8,128]{1,0:T(8,128)S(1)}, u32[]{:S(2)}, u32[]{:S(2)}) collective-permute-start(f32[8,128]{1,0:T(8,128)S(1)} %add.28), channel_id=1, source_target_pairs={{0,96},{16,112},{32,64},{48,80},{64,32},{80,48},{96,0},{112,16},{1... | collective-permute-start | bytes 12296 | tf_op jit(solution)/shard_map/ppermute | solution.py:567
  18.0 20.0 %collective-permute-start.8 = (f32[8,128]{1,0:T(8,128)S(1)}, f32[8,128]{1,0:T(8,128)S(1)}, u32[]{:S(2)}, u32[]{:S(2)}) collective-permute-start(f32[8,128]{1,0:T(8,128)S(1)} %add.28), channel_id=1, source_target_pairs={{0,32},{16,48},{32,0},{48,16},{64,96},{80,112},{96,64},{112,80},{1... | collective-permute-start | bytes 12296 | tf_op jit(solution)/shard_map/ppermute | solution.py:567
  18.0 20.0 %collective-permute-start.7 = (f32[8,128]{1,0:T(8,128)S(1)}, f32[8,128]{1,0:T(8,128)S(1)}, u32[]{:S(2)}, u32[]{:S(2)}) collective-permute-start(f32[8,128]{1,0:T(8,128)S(1)} %add.28), channel_id=1, source_target_pairs={{0,64},{16,80},{32,96},{48,112},{64,0},{80,16},{96,32},{112,48},{1... | collective-permute-start | bytes 12296 | tf_op jit(solution)/shard_map/ppermute | solution.py:567

commit v3 on v2

--- a/solution.py
+++ b/solution.py
@@ -20,7 +20,7 @@
 JUMP = 512.0
 BLOCK = 16
 GROUP = 10
-JOBS = 8
+JOBS = 6
 DEPTH = 256
 WAYS = 6
 START = 3
@@ -428,8 +428,10 @@
     b_out[TILE:, TILE:] = jnp.zeros_like(wl)
 
 
-def apply_kernel(b, own, own_weights, rest, rest_weights, root, root_weights, out_hbm, ready, out_sems, *, accs):
+def apply_kernel(b, u, own, own_weights, rest, rest_weights, root, root_weights, out_hbm, u_hbm, ready, out_sems, u_sem, *, accs):
     tiles = root.shape[0] // TILE
+    u_copy = pltpu.make_async_copy(u, u_hbm, u_sem)
+    u_copy.start()
     early = own.shape[0] // TILE
     is_root = lax.axis_index("col") == 0
 
@@ -476,6 +478,7 @@
         return carry
 
     lax.fori_loop(0, tiles // WAYS, finish, 0)
+    u_copy.wait()
 
 
 def vmem():
@@ -582,7 +585,7 @@
         compiler_params=limit(20),
         name="rest",
     )(stay(own_counts), lhs, root_message, own_tab, own_side)
-    factors, u_rows = pl.pallas_call(
+    factors, upper_rows = pl.pallas_call(
         solve_kernel,
         out_shape=(
             jax.ShapeDtypeStruct((2 * TILE, 2 * TILE), BF),
@@ -598,16 +601,22 @@
         compiler_params=limit(8),
         name="solve",
     )(picked, own_tab, own_side, root_tab, root_side)
-    factored = pl.pallas_call(
+    return pl.pallas_call(
         functools.partial(apply_kernel, accs=accs),
-        out_shape=jax.ShapeDtypeStruct((local_rows, TILE), F32),
-        in_specs=[vmem()] * 7,
-        out_specs=hbm(),
-        scratch_shapes=[pltpu.VMEM((local_rows, TILE), F32), pltpu.SemaphoreType.DMA((tiles // WAYS,))],
+        out_shape=(
+            jax.ShapeDtypeStruct((local_rows, TILE), F32),
+            jax.ShapeDtypeStruct((TILE, TILE), F32),
+        ),
+        in_specs=[vmem()] * 8,
+        out_specs=(hbm(), hbm()),
+        scratch_shapes=[
+            pltpu.VMEM((local_rows, TILE), F32),
+            pltpu.SemaphoreType.DMA((tiles // WAYS,)),
+            pltpu.SemaphoreType.DMA,
+        ],
         compiler_params=limit(20),
         name="apply",
-    )(factors, own_sum, own_weights, rest_sum, rest_weights, root_sum, root_weights)
-    return factored, u_rows
+    )(factors, upper_rows, own_sum, own_weights, rest_sum, rest_weights, root_sum, root_weights)
 
 
 def body(accs, *args):

time: 45.3 us -> 45 us (level)
    pallas_call x1, Pallas kernels: 4.72 us -> 4.25 us  [steps(): pl.pallas_call(solve_kernel, out_shape=(jax.ShapeDtypeStruct((2 * TILE, 2...]
where the time goes in v3:
time: 45 us; the launch traced here: 44.8 us
  Pallas kernels  34.2 us (76%)
  starting transfers between devices  8.48 us (19%)
  waiting for transfers between devices  1.18 us (3%)
  between operations  0.83 us (2%)
    pallas_call x1, Pallas kernels, steps(): pl.pallas_call(functools.partial(rest_kernel, accs=accs), out_shape=(part...  16.2 us
    pallas_call x1, Pallas kernels, steps(): pl.pallas_call(functools.partial(own_kernel, accs=accs), out_shape=(part(...  10.3 us
    pallas_call x1, Pallas kernels, steps(): pl.pallas_call(solve_kernel, out_shape=(jax.ShapeDtypeStruct((2 * TILE, 2...  4.25 us
    ppermute x3, starting transfers between devices, steps(): lax.ppermute(picked, 'row', [(i, i ^ k) for i in range(8)])  3.85 us
    ppermute x3, starting transfers between devices, steps(): lax.ppermute(y_part, 'col', [(i, i + k) for i in range(4)])  2.62 us
    pallas_call x1, Pallas kernels, steps(): pl.pallas_call(functools.partial(apply_kernel, accs=accs), out_shape=(jax...  2.38 us
    ppermute x3, starting transfers between devices, steps(): got = numbered(lambda k: lax.ppermute(message, 'col', [(0, k)]), (2, 3, 1))  1.98 us
    ppermute x1, waiting for transfers between devices, steps(): lax.ppermute(picked, 'row', [(i, i ^ 1) for i in range(8)])  1.15 us
  transfers between devices with their start and end apart: 10, of which 1 were waited for; matrix products, arithmetic and copies ran while one was open for 0% of the time, Pallas kernels for 59%

profile of v3, /device:TPU:27, one launch (start us, length us, event | category | flops | bytes accessed | tf_op | source)
XLA Modules:
  0.0 44.8 jit_solution(17770557475125021273)
XLA Ops:
  0.6 1.0 %pack.1 = (f32[8,128]{1,0:T(8,128)S(1)}, f32[3,7680]{1,0:T(4,128)S(1)}, s32[60,128]{1,0:T(8,128)S(1)}, s32[1,128]{1,0:T(1,128)S(1)}) custom-call(f32[4,128]{1,0:T(4,128)} %sources_hbm.1, s32[1,60]{1,0:T(1,128)} %bitcast.5, f32[3,7680]{1,0:T(4,128)} %points_hbm.1, s32[60,128]{1,0:T(8,128)} %bitcast.4, s32[1,128]{1,0:T(1,128)} %bitcast.8), custom_call_target="tpu_custom_call" | custom-call | tf_op jit(solution)/shard_map/pack/pallas_call | solution.py:528
  1.6 0.7 %collective-permute-start.2 = (f32[8,128]{1,0:T(8,128)S(1)}, f32[8,128]{1,0:T(8,128)S(1)}, u32[]{:S(2)}, u32[]{:S(2)}) collective-permute-start(f32[8,128]{1,0:T(8,128)S(1)} %get-tuple-element.23.message), channel_id=1, source_target_pairs={{0,1},{16,17},{32,33},{48,49},{64,65},{80,81},{96,97},{112,113}} | collective-permute-start | bytes 12296 | tf_op jit(solution)/shard_map/ppermute | solution.py:548
  2.3 0.7 %collective-permute-start.1 = (f32[8,128]{1,0:T(8,128)S(1)}, f32[8,128]{1,0:T(8,128)S(1)}, u32[]{:S(2)}, u32[]{:S(2)}) collective-permute-start(f32[8,128]{1,0:T(8,128)S(1)} %get-tuple-element.23.message), channel_id=1, source_target_pairs={{0,3},{16,19},{32,35},{48,51},{64,67},{80,83},{96,99},{112,115}} | collective-permute-start | bytes 12296 | tf_op jit(solution)/shard_map/ppermute | solution.py:548
  3.0 0.7 %collective-permute-start = (f32[8,128]{1,0:T(8,128)S(1)}, f32[8,128]{1,0:T(8,128)S(1)}, u32[]{:S(2)}, u32[]{:S(2)}) collective-permute-start(f32[8,128]{1,0:T(8,128)S(1)} %get-tuple-element.23.message), channel_id=1, source_target_pairs={{0,2},{16,18},{32,34},{48,50},{64,66},{80,82},{96,98},{112,114}} | collective-permute-start | bytes 12296 | tf_op jit(solution)/shard_map/ppermute | solution.py:548
  3.6 0.0 collective-permute-done.2
  3.6 0.0 collective-permute-done.1
  3.7 0.0 collective-permute-done
  3.7 1.3 %collective-permute-start.5 = (f32[8,128]{1,0:T(8,128)S(1)}, f32[8,128]{1,0:T(8,128)S(1)}, u32[]{:S(2)}, u32[]{:S(2)}) collective-permute-start(f32[8,128]{1,0:T(8,128)S(1)} %add_select_fusion.1), channel_id=1, source_target_pairs={{0,4},{1,5},{2,6},{3,7},{16,20},{17,21},{18,22},{19,23},{32,36},{3... | collective-permute-start | bytes 12296 | tf_op jit(solution)/shard_map/ppermute | solution.py:550
  5.0 0.7 %collective-permute-start.4 = (f32[8,128]{1,0:T(8,128)S(1)}, f32[8,128]{1,0:T(8,128)S(1)}, u32[]{:S(2)}, u32[]{:S(2)}) collective-permute-start(f32[8,128]{1,0:T(8,128)S(1)} %add_select_fusion.1), channel_id=1, source_target_pairs={{0,12},{1,13},{2,14},{3,15},{16,28},{17,29},{18,30},{19,31},{32,44... | collective-permute-start | bytes 12296 | tf_op jit(solution)/shard_map/ppermute | solution.py:550
  5.7 0.7 %collective-permute-start.3 = (f32[8,128]{1,0:T(8,128)S(1)}, f32[8,128]{1,0:T(8,128)S(1)}, u32[]{:S(2)}, u32[]{:S(2)}) collective-permute-start(f32[8,128]{1,0:T(8,128)S(1)} %add_select_fusion.1), channel_id=1, source_target_pairs={{0,8},{1,9},{2,10},{3,11},{16,24},{17,25},{18,26},{19,27},{32,40},... | collective-permute-start | bytes 12296 | tf_op jit(solution)/shard_map/ppermute | solution.py:550
  6.3 10.3 %own.1 = (f32[3840,128]{1,0:T(8,128)S(1)}, f32[30,128]{1,0:T(8,128)S(1)}, bf16[7680,128]{1,0:T(8,128)(2,1)S(1)}, bf16[8,32,256]{2,1,0:T(8,128)(2,1)S(1)}, bf16[3...) custom-call(s32[60]{0:T(128)} %bitcast.6, f32[3,7680]{1,0:T(4,128)S(1)} %get-tuple-element.20.points, ...), custom_call_target="tpu_custom_call" | custom-call | tf_op jit(solution)/shard_map/own/pallas_call | solution.py:552
  16.7 0.0 collective-permute-done.5
  16.7 0.0 collective-permute-done.4
  16.7 0.0 collective-permute-done.3
  16.7 0.1 pick.1
  16.8 0.0 collective-permute-start.6
  16.8 1.2 %collective-permute-done.6 = f32[8,128]{1,0:T(8,128)S(1)} collective-permute-done((f32[8,128]{1,0:T(8,128)S(1)}, f32[8,128]{1,0:T(8,128)S(1)}, u32[]{:S(2)}, u32[]{:S(2)}) %collective-permute-start.6) | collective-permute-done | bytes 4128 | tf_op jit(solution)/shard_map/ppermute | solution.py:569
  18.0 0.0 collective-permute-start.9
  18.0 0.0 collective-permute-start.8
  18.0 3.8 %collective-permute-start.7 = (f32[8,128]{1,0:T(8,128)S(1)}, f32[8,128]{1,0:T(8,128)S(1)}, u32[]{:S(2)}, u32[]{:S(2)}) collective-permute-start(f32[8,128]{1,0:T(8,128)S(1)} %add.28), channel_id=1, source_target_pairs={{0,64},{16,80},{32,96},{48,112},{64,0},{80,16},{96,32},{112,48},{1... | collective-permute-start | bytes 12296 | tf_op jit(solution)/shard_map/ppermute | solution.py:570
  21.8 16.2 %rest.1 = (f32[3840,128]{1,0:T(8,128)S(1)}, f32[30,128]{1,0:T(8,128)S(1)}, f32[7680,128]{1,0:T(8,128)S(1)}, f32[60,128]{1,0:T(8,128)S(1)}, bf16[8,32,256]{2,1,0:T(8,128)(2,1)S(1)}, /*index=5*/bf16[32,256]{1,0:T(8,128)(2,1)S(1)}) custom-call(s32[60]{0:T(128)} %bitcast.7, bf16[7680,128]{1,0:T(8,128)(2,1)S(1)} %get-tuple-element.27.lhs, ...), custom_call_target="tpu_custom_call" | custom-call | tf_op jit(solution)/shard_map/rest/pallas_call | solution.py:572
  38.1 0.0 collective-permute-done.9
  38.1 0.0 collective-permute-done.8
  38.1 0.0 collective-permute-done.7
  38.1 4.2 %solve.1 = (bf16[256,256]{1,0:T(8,128)(2,1)S(1)}, f32[128,128]{1,0:T(8,128)S(1)}) custom-call(f32[8,128]{1,0:T(8,128)S(1)} %add_add_fusion.picked, bf16[8,32,256]{2,1,0:T(8,128)(2,1)S(1)} %get-tuple-element.25.own_tab, bf16[32,256]{1,0:T(8,128)(2,1)S(1)} %get-tuple-element.26.own_side, bf16[8,32,256]{2,1,0:T(8,128)(2,1)S(1)} %get-tuple-element.28.root_tab, ...), custom_call_target="tpu_custom_call" | custom-call | tf_op jit(solution)/shard_map/solve/pallas_call | solution.py:588
  42.4 2.4 %apply.1 = (f32[7680,128]{1,0:T(8,128)}, f32[128,128]{1,0:T(8,128)}) custom-call(bf16[256,256]{1,0:T(8,128)(2,1)S(1)} %get-tuple-element.30.b, f32[128,128]{1,0:T(8,128)S(1)} %get-tuple-element.31.u, f32[3840,128]{1,0:T(8,128)S(1)} %get-tuple-element.32.own, f32[30,128]{1,0:T(8,128)S(1)} %get-tuple-element.33.own_weights, ...), custom_call_target="tpu_custom_call" | custom-call | tf_op jit(solution)/shard_map/apply/pallas_call | solution.py:604
  (4 shorter events, 0.0 us)
Async XLA Ops:
  1.6 2.0 %collective-permute-start.2 = (f32[8,128]{1,0:T(8,128)S(1)}, f32[8,128]{1,0:T(8,128)S(1)}, u32[]{:S(2)}, u32[]{:S(2)}) collective-permute-start(f32[8,128]{1,0:T(8,128)S(1)} %get-tuple-element.23.message), channel_id=1, source_target_pairs={{0,1},{16,17},{32,33},{48,49},{64,65},{80,81},{96,97},{112,113}} | collective-permute-start | bytes 12296 | tf_op jit(solution)/shard_map/ppermute | solution.py:548
  2.3 1.4 %collective-permute-start.1 = (f32[8,128]{1,0:T(8,128)S(1)}, f32[8,128]{1,0:T(8,128)S(1)}, u32[]{:S(2)}, u32[]{:S(2)}) collective-permute-start(f32[8,128]{1,0:T(8,128)S(1)} %get-tuple-element.23.message), channel_id=1, source_target_pairs={{0,3},{16,19},{32,35},{48,51},{64,67},{80,83},{96,99},{112,115}} | collective-permute-start | bytes 12296 | tf_op jit(solution)/shard_map/ppermute | solution.py:548
  3.0 0.7 %collective-permute-start = (f32[8,128]{1,0:T(8,128)S(1)}, f32[8,128]{1,0:T(8,128)S(1)}, u32[]{:S(2)}, u32[]{:S(2)}) collective-permute-start(f32[8,128]{1,0:T(8,128)S(1)} %get-tuple-element.23.message), channel_id=1, source_target_pairs={{0,2},{16,18},{32,34},{48,50},{64,66},{80,82},{96,98},{112,114}} | collective-permute-start | bytes 12296 | tf_op jit(solution)/shard_map/ppermute | solution.py:548
  3.7 13.0 %collective-permute-start.5 = (f32[8,128]{1,0:T(8,128)S(1)}, f32[8,128]{1,0:T(8,128)S(1)}, u32[]{:S(2)}, u32[]{:S(2)}) collective-permute-start(f32[8,128]{1,0:T(8,128)S(1)} %add_select_fusion.1), channel_id=1, source_target_pairs={{0,4},{1,5},{2,6},{3,7},{16,20},{17,21},{18,22},{19,23},{32,36},{3... | collective-permute-start | bytes 12296 | tf_op jit(solution)/shard_map/ppermute | solution.py:550
  5.0 11.7 %collective-permute-start.4 = (f32[8,128]{1,0:T(8,128)S(1)}, f32[8,128]{1,0:T(8,128)S(1)}, u32[]{:S(2)}, u32[]{:S(2)}) collective-permute-start(f32[8,128]{1,0:T(8,128)S(1)} %add_select_fusion.1), channel_id=1, source_target_pairs={{0,12},{1,13},{2,14},{3,15},{16,28},{17,29},{18,30},{19,31},{32,44... | collective-permute-start | bytes 12296 | tf_op jit(solution)/shard_map/ppermute | solution.py:550
  5.7 11.0 %collective-permute-start.3 = (f32[8,128]{1,0:T(8,128)S(1)}, f32[8,128]{1,0:T(8,128)S(1)}, u32[]{:S(2)}, u32[]{:S(2)}) collective-permute-start(f32[8,128]{1,0:T(8,128)S(1)} %add_select_fusion.1), channel_id=1, source_target_pairs={{0,8},{1,9},{2,10},{3,11},{16,24},{17,25},{18,26},{19,27},{32,40},... | collective-permute-start | bytes 12296 | tf_op jit(solution)/shard_map/ppermute | solution.py:550
  16.8 1.2 %collective-permute-start.6 = (f32[8,128]{1,0:T(8,128)S(1)}, f32[8,128]{1,0:T(8,128)S(1)}, u32[]{:S(2)}, u32[]{:S(2)}) collective-permute-start(f32[8,128]{1,0:T(8,128)S(1)} %pick.1), channel_id=1, source_target_pairs={{0,16},{16,0},{32,48},{48,32},{64,80},{80,64},{96,112},{112,96},{1... | collective-permute-start | bytes 12296 | tf_op jit(solution)/shard_map/ppermute | solution.py:569
  18.0 20.1 %collective-permute-start.9 = (f32[8,128]{1,0:T(8,128)S(1)}, f32[8,128]{1,0:T(8,128)S(1)}, u32[]{:S(2)}, u32[]{:S(2)}) collective-permute-start(f32[8,128]{1,0:T(8,128)S(1)} %add.28), channel_id=1, source_target_pairs={{0,96},{16,112},{32,64},{48,80},{64,32},{80,48},{96,0},{112,16},{1... | collective-permute-start | bytes 12296 | tf_op jit(solution)/shard_map/ppermute | solution.py:570
  18.0 20.1 %collective-permute-start.8 = (f32[8,128]{1,0:T(8,128)S(1)}, f32[8,128]{1,0:T(8,128)S(1)}, u32[]{:S(2)}, u32[]{:S(2)}) collective-permute-start(f32[8,128]{1,0:T(8,128)S(1)} %add.28), channel_id=1, source_target_pairs={{0,32},{16,48},{32,0},{48,16},{64,96},{80,112},{96,64},{112,80},{1... | collective-permute-start | bytes 12296 | tf_op jit(solution)/shard_map/ppermute | solution.py:570
  18.0 20.1 %collective-permute-start.7 = (f32[8,128]{1,0:T(8,128)S(1)}, f32[8,128]{1,0:T(8,128)S(1)}, u32[]{:S(2)}, u32[]{:S(2)}) collective-permute-start(f32[8,128]{1,0:T(8,128)S(1)} %add.28), channel_id=1, source_target_pairs={{0,64},{16,80},{32,96},{48,112},{64,0},{80,16},{96,32},{112,48},{1... | collective-permute-start | bytes 12296 | tf_op jit(solution)/shard_map/ppermute | solution.py:570
